TPU v7x, 32 devices: a whole 2x2x4 slice. The times are simulated.
32 devices in a mesh: batch: 8 (over z, x), rep: 4 (over y, core).
Axes of the slice: x: 2, y: 2, z: 4, core: 2. Of those that a mesh axis runs over, the one named last changes fastest.
Arguments:
- latents: bfloat16 [4, 16, 512, 1024], P('rep', 'batch'), may hold values from -6 to 6
- query_key_value_weight: bfloat16 [1024, 3072], P('batch'), may hold values from -0.1875 to 0.1875
- output_weight: bfloat16 [1024, 1024], P('batch'), may hold values from -1.5 to 1.5
- up_weight: bfloat16 [1024, 1024], P('batch'), may hold values from -0.1875 to 0.1875
- down_weight: bfloat16 [1024, 1024], P('batch'), may hold values from -0.1875 to 0.1875
- norm_gains: bfloat16 [2, 1024], P(None, 'batch'), may hold values from 0.099609375 to 1.8984375
- biases: bfloat16 [6, 1024], P(None, 'batch'), may hold values from -1.5 to 1.5
- feed_forward_bias: bfloat16 [1024], P('batch'), may hold values from -1.5 to 1.5
- cotangent: bfloat16 [4, 16, 512, 1024], P('rep', 'batch'), may hold values from -6 to 6
Outputs:
- out_latents: bfloat16 [4, 16, 512, 1024], P('rep', 'batch')
- grad_latents: bfloat16 [4, 16, 512, 1024], P('rep', 'batch')
- grad_w_qkv: float32 [1024, 3072], P('batch')
- grad_w_out: float32 [1024, 1024], P('batch')
- grad_w_up: float32 [1024, 1024], P('batch')
- grad_w_down: float32 [1024, 1024], P('batch')
- grad_gains: float32 [2, 1024], P(None, 'batch')
- grad_biases: float32 [6, 1024], P(None, 'batch')
- grad_mlp_bias: float32 [1024], P('batch')
All inputs are finite; a program needn't handle non-finite values.
Results may differ from a plain program's by a relative error of at most 0.014.
The roundings to bfloat16 on the way count: a program that leaves them out, or rounds other values in their place, can miss the bound.
Values may be sent and summed in bfloat16 or wider, within the bound.
No kernel may reach another device: no remote copies, remote signals or barrier semaphores. Data moves between devices by JAX's collectives and lax.ppermute only.
A program may use at most 192 MiB of HBM per device.

v0:
```python
import jax
import jax.numpy as jnp
from jax import lax
from jax.sharding import PartitionSpec as P

HEADS = 8
EPS = 1e-05
AXES = ("batch", "rep")
BF = jnp.bfloat16
F32 = jnp.float32


def layer_norm(values, gain, shift):
    mean = jnp.mean(values, axis=-1, keepdims=True)
    centred = values - mean
    spread = jnp.mean(centred * centred, axis=-1, keepdims=True)
    return centred * lax.rsqrt(spread + EPS) * gain + shift


def permutation(move, nb, nr):
    pairs = []
    for b in range(nb):
        for r in range(nr):
            tb, tr = move(b, r)
            pairs.append((b * nr + r, tb * nr + tr))
    return pairs


class Links:

    def __init__(self, nb, nr):

        def swap(kb, kr):
            return permutation(lambda b, r: (b ^ kb, r ^ kr), nb, nr)

        self.core = swap(0, 1)
        self.rep = [swap(0, 1), swap(0, 2), swap(0, 3)]
        self.z = [swap(2, 0), swap(4, 0), swap(6, 0)]
        self.y_or_x = permutation(lambda b, r: (b, r ^ 2) if r % 2 == 0 else (b ^ 1, r), nb, nr)
        self.x_or_y = permutation(lambda b, r: (b ^ 1, r) if r % 2 == 0 else (b, r ^ 2), nb, nr)
        batch, rep = (lax.axis_index("batch"), lax.axis_index("rep"))
        self.xi, self.zi = (batch % 2, batch // 2)
        self.ci, self.yi = (rep % 2, rep // 2)


def move(value, pairs):
    return lax.ppermute(value, AXES, pairs)


def flip_if(bit, value, axis):
    return jnp.where(bit == 1, jnp.flip(value, axis), value)


def gather_rows(local, links):
    rows, n = local.shape
    quarter = lax.dynamic_index_in_dim(
        local.reshape(4, rows // 4, n), links.ci * 2 + links.yi, 0, keepdims=False
    )
    own = jnp.stack([quarter] + [move(quarter, p) for p in links.z])
    first = move(own, links.y_or_x)
    second = move(own, links.x_or_y)
    third = move(first, links.x_or_y)
    halves = []
    here = [own, first, second, third]
    there = [move(part, links.core) for part in here]
    for parts, core in ((here, links.ci), (there, 1 - links.ci)):
        a, f, s, t = parts
        dx = jnp.where(core == 1, f, s)
        dy = jnp.where(core == 1, s, f)
        halves.append(jnp.stack([jnp.stack([a, dy]), jnp.stack([dx, t])]))
    whole = jnp.stack(halves)
    whole = flip_if(links.ci, whole, 0)
    whole = flip_if(links.xi, whole, 1)
    whole = flip_if(links.yi, whole, 2)
    whole = flip_if(links.zi % 2, whole.reshape(2, 2, 2, 2, 2, rows // 4, n), 4)
    whole = flip_if(links.zi // 2, whole, 3)
    whole = whole.transpose(3, 4, 1, 0, 2, 5, 6)
    return whole.reshape(8 * rows, n)


def reduce_rows(partial, links):
    total, n = partial.shape
    rows, q = (total // 8, n // 4)
    view = partial.reshape(4, 2, rows, 2, 2, q)
    view = view.transpose(3, 1, 4, 0, 2, 5)
    keep = lax.dynamic_index_in_dim(view, links.ci, 0, keepdims=False)
    send = lax.dynamic_index_in_dim(view, 1 - links.ci, 0, keepdims=False).astype(BF)
    held = keep + move(send, links.core).astype(F32)
    held = jnp.where(links.ci == 0, held, held.transpose(1, 0, 2, 3, 4))
    mine = jnp.where(links.ci == 0, links.xi, links.yi)
    keep = lax.dynamic_index_in_dim(held, mine, 0, keepdims=False)
    send = lax.dynamic_index_in_dim(held, 1 - mine, 0, keepdims=False).astype(BF)
    held = keep + move(send, links.x_or_y).astype(F32)
    mine = jnp.where(links.ci == 0, links.yi, links.xi)
    keep = lax.dynamic_index_in_dim(held, mine, 0, keepdims=False)
    send = lax.dynamic_index_in_dim(held, 1 - mine, 0, keepdims=False).astype(BF)
    held = keep + move(send, links.y_or_x).astype(F32)
    out = lax.dynamic_index_in_dim(held, links.zi, 0, keepdims=False)
    for k, pairs in enumerate(links.z):
        send = lax.dynamic_index_in_dim(held, links.zi ^ k + 1, 0, keepdims=False).astype(BF)
        out = out + move(send, pairs).astype(F32)
    out = out.astype(BF)
    by_core, by_y, by_both = [move(out, p) for p in links.rep]
    grid = jnp.stack([jnp.stack([out, by_y]), jnp.stack([by_core, by_both])])
    grid = flip_if(links.yi, flip_if(links.ci, grid, 0), 1)
    return grid.transpose(2, 0, 1, 3).reshape(rows, n).astype(F32)


def heads_of(packed):
    images, length, width = packed.shape
    size = width // 3 // HEADS
    view = packed.reshape(images, length, 3, HEADS, size)
    return (view[:, :, 0], view[:, :, 1], view[:, :, 2], size ** (-0.5))


def per_device(latents, w_qkv, w_out, w_up, w_down, gains, biases, ff_bias, cotangent, *, nb, nr):
    reps, images, length, width = latents.shape
    x = latents.reshape(-1, width).astype(F32)
    cot = cotangent.reshape(-1, width)
    count = reps * images
    small = jnp.concatenate([gains, biases, ff_bias[None]], axis=0)
    native = nb != 8 or nr != 4
    if native:
        small = lax.all_gather(small, "batch", axis=1, tiled=True)
        w_qkv, w_out, w_up, w_down = (
            lax.all_gather(w, "batch", axis=0, tiled=True) for w in (w_qkv, w_out, w_up, w_down)
        )
    else:
        links = Links(nb, nr)
        small = lax.all_gather(small, "batch", axis=1, tiled=True)
        w_qkv = gather_rows(w_qkv, links)
        rest = gather_rows(jnp.concatenate([w_out, w_up, w_down], axis=1), links)
        w_out, w_up, w_down = (rest[:, :width], rest[:, width:-width], rest[:, -width:])
    small = small.astype(F32)
    g1, g2 = (small[0], small[1])
    b1, bq, bv, bo, b2, bd, bu = (small[i] for i in range(2, 9))

    def dot(a, b, dims):
        return lax.dot_general(a, b, (dims, ((), ())), preferred_element_type=F32)

    NN, NT, TN = (((1,), (0,)), ((1,), (1,)), ((0,), (0,)))
    first, pull_one = jax.vjp(layer_norm, x, g1, b1)
    first = first.astype(BF)
    packed = dot(first, w_qkv, NN) + jnp.concatenate([bq, jnp.zeros_like(bq), bv])
    packed = packed.astype(BF).reshape(count, length, 3 * width)
    q, k, v, scale = heads_of(packed)
    scores = jnp.einsum("iqhd,ikhd->ihqk", q, k, preferred_element_type=F32) * scale
    top = jnp.max(scores, axis=-1, keepdims=True)
    raised = jnp.exp(scores - top)
    p = raised / jnp.sum(raised, axis=-1, keepdims=True)
    probs = p.astype(BF)
    mixed = jnp.einsum("ihqk,ikhd->iqhd", probs, v, preferred_element_type=F32)
    mixed = mixed.astype(BF).reshape(-1, width)
    middle = x + dot(mixed, w_out, NN) + bo
    second, pull_two = jax.vjp(layer_norm, middle, g2, b2)
    second = second.astype(BF)
    hidden = dot(second, w_up, NN) + bu
    active, pull_gelu = jax.vjp(jax.nn.gelu, hidden)
    active = active.astype(BF)
    out = (middle + dot(active, w_down, NN) + bd).astype(BF)
    gw_down = dot(active, cot, TN)
    gb_down = jnp.sum(cot.astype(F32), axis=0)
    g_hidden = pull_gelu(dot(cot, w_down, NT))[0].astype(BF)
    gw_up = dot(second, g_hidden, TN)
    gb_up = jnp.sum(g_hidden.astype(F32), axis=0)
    g_mid, gg2, gb2 = pull_two(dot(g_hidden, w_up, NT))
    g_middle = cot.astype(F32) + g_mid
    g_attn = g_middle.astype(BF)
    gw_out = dot(mixed, g_attn, TN)
    gb_out = jnp.sum(g_attn.astype(F32), axis=0)
    g_mixed = dot(g_attn, w_out, NT).astype(BF).reshape(count, length, HEADS, -1)
    g_v = jnp.einsum("ihqk,iqhd->ikhd", probs, g_mixed, preferred_element_type=F32)
    g_p = jnp.einsum("iqhd,ikhd->ihqk", g_mixed, v, preferred_element_type=F32)
    g_s = (p * (g_p - jnp.sum(g_p * p, axis=-1, keepdims=True))).astype(BF)
    g_q = jnp.einsum("ihqk,ikhd->iqhd", g_s, k, preferred_element_type=F32) * scale
    g_k = jnp.einsum("ihqk,iqhd->ikhd", g_s, q, preferred_element_type=F32) * scale
    g_packed = jnp.stack([g_q, g_k, g_v], axis=2).astype(BF).reshape(-1, 3 * width)
    gw_qkv = dot(first, g_packed, TN)
    gb_packed = jnp.sum(g_packed.astype(F32), axis=0)
    g_in, gg1, gb1 = pull_one(dot(g_packed, w_qkv, NT))
    g_lat = (g_middle + g_in).astype(BF)
    zero = jnp.zeros_like(gb_up)
    smalls = jnp.stack(
        [gg1, gg2, gb1, gb_packed[:width], gb_packed[2 * width :], gb_out, gb2, gb_down, gb_up]
        + [zero] * 7
    )
    smalls = lax.psum(smalls, AXES)
    smalls = lax.dynamic_slice_in_dim(
        smalls, lax.axis_index("batch") * (width // nb), width // nb, 1
    )
    if native:

        def reduced(g):
            g = lax.psum_scatter(g, "batch", scatter_dimension=0, tiled=True)
            return lax.psum(g.astype(BF), "rep").astype(F32)

        gw_qkv, gw_out, gw_up, gw_down = (reduced(g) for g in (gw_qkv, gw_out, gw_up, gw_down))
    else:
        rest = reduce_rows(jnp.concatenate([gw_out, gw_up, gw_down], axis=1), links)
        gw_qkv = reduce_rows(gw_qkv, links)
        gw_out, gw_up, gw_down = (rest[:, :width], rest[:, width:-width], rest[:, -width:])
    return (
        out.reshape(latents.shape),
        g_lat.reshape(latents.shape),
        gw_qkv,
        gw_out,
        gw_up,
        gw_down,
        smalls[:2],
        smalls[2:8],
        smalls[8],
    )


def solution(mesh):
    nb, nr = (mesh.shape["batch"], mesh.shape["rep"])

    def body(*args):
        return per_device(*args, nb=nb, nr=nr)

    rows = P("batch", None)
    cols = P(None, "batch")
    data = P("rep", "batch", None, None)
    return jax.shard_map(
        body,
        mesh=mesh,
        in_specs=(data, rows, rows, rows, rows, cols, cols, P("batch"), data),
        out_specs=(data, data, rows, rows, rows, rows, cols, cols, P("batch")),
        check_vma=False,
    )
```

profile of v0, /device:TPU:0, one launch (start us, length us, event | category | flops | bytes accessed | tf_op | source)
XLA Modules:
  0.0 650.0 jit_solution(16085910962180508302)
XLA Ops:
  8.3 5.1 collective-permute-start.2
  20.9 45.8 %all_gather.3 = bf16[9,1024]{1,0:T(8,128)(2,1)S(1)} all-gather(bf16[9,128]{1,0:T(8,128)(2,1)S(1)} %pad_maximum_fusion.9), channel_id=1, replica_groups=mesh['batch'=8,'rep'=4] {'batch'}, dimensions={1}, use_global_device_ids=true | all-gather | bytes 20736 | tf_op jit(solution)/shard_map/all_gather | solution.py:130
  77.2 7.4 %collective-permute-done.4 = bf16[4,32,3072]{2,1,0:T(8,128)(2,1)} collective-permute-done((bf16[4,32,3072]{2,1,0:T(8,128)(2,1)}, bf16[4,32,3072]{2,1,0:T(8,128)(2,1)}, u32[]{:S(2)}, u32[]{:S(2)}) %collective-permute-start.4) | collective-permute-done | bytes 786464 | tf_op jit(solution)/shard_map/ppermute | solution.py:47
  89.4 12.0 %collective-permute-done.14 = bf16[4,32,3072]{2,1,0:T(8,128)(2,1)S(1)} collective-permute-done((bf16[4,32,3072]{2,1,0:T(8,128)(2,1)S(1)}, bf16[4,32,3072]{2,1,0:T(8,128)(2,1)S(1)}, u32[]{:S(2)}, u32[]{:S(2)}) %collective-permute-start.14) | collective-permute-done | bytes 786464 | tf_op jit(solution)/shard_map/ppermute | solution.py:47
  107.8 8.4 %collective-permute-done.15 = bf16[4,32,3072]{2,1,0:T(8,128)(2,1)} collective-permute-done((bf16[4,32,3072]{2,1,0:T(8,128)(2,1)S(1)}, bf16[4,32,3072]{2,1,0:T(8,128)(2,1)}, u32[]{:S(2)}, u32[]{:S(2)}) %collective-permute-start.15) | collective-permute-done | bytes 786464 | tf_op jit(solution)/shard_map/ppermute | solution.py:47
  130.7 7.5 %reverse_select_fusion.4 = bf16[2,2,2,4,32,3072]{5,4,3,2,1,0:T(8,128)(2,1)S(1)} fusion(bf16[2,2,2,4,32,3072]{5,4,3,2,1,0:T(8,128)(2,1)} %pad_maximum_fusion.2, pred[]{:T(512)S(6)} %eq.23), kind=kLoop, calls=%fused_computation.14 | loop fusion | flops 3145728 | bytes 12582913 | tf_op jit(solution)/shard_map/jit(_where)/select_n | solution.py:51
  138.2 4.4 reverse_select_fusion.8
  142.6 4.4 reverse_select_fusion.3
  147.0 7.6 %reverse_select_fusion.7 = bf16[2,2,2,4,32,3072]{5,4,2,0,1,3:T(8,128)(2,1)S(1)} fusion(bf16[2,2,2,4,32,3072]{5,4,2,0,1,3:T(8,128)(2,1)} %reverse_select_fusion.8, pred[]{:T(512)S(6)} %eq.21), kind=kLoop, calls=%fused_computation.17 | loop fusion | flops 3145728 | bytes 12582913 | tf_op jit(solution)/shard_map/jit(_where)/select_n | solution.py:51
  154.7 4.4 reverse_select_fusion.2
  162.4 4.8 reverse_select_fusion.6
  169.0 7.5 %reverse_select_fusion.5 = bf16[2,2,2,2,2,32,3072]{6,5,2,0,1,4,3:T(8,128)(2,1)S(1)} fusion(bf16[2,2,2,2,2,32,3072]{6,5,2,0,1,4,3:T(8,128)(2,1)} %reverse_select_fusion.6, pred[]{:T(512)S(6)} %eq.19), kind=kLoop, calls=%fused_computation.15 | loop fusion | flops 3145728 | bytes 12582913 | tf_op jit(solution)/shard_map/jit(_where)/select_n | solution.py:51
  176.5 4.4 reverse_select_fusion
  181.3 8.6 %fusion.5 = bf16[128,8,24,128]{3,1,2,0:T(8,128)(2,1)} fusion(f32[3072]{0:T(1024)S(1)} %pad_maximum_fusion.8, bf16[1024,1024]{1,0:T(8,128)(2,1)S(1)} %bitcast.349, bf16[1024,3072]{1,0:T(8,128)(2,1)S(1)} %bitcast.343), kind=kOutput, calls=%fused_computation.22 | convolution fusion | flops 6448742400 | bytes 14692352 | tf_op jit(solution)/shard_map/dot_general | solution.py:139
  189.9 4.7 copy.92
  197.7 4.6 copy.84
  202.3 10.4 %fusion.52 = f32[2,8,512,512]{2,3,1,0:T(8,128)} fusion(bf16[2,512,1,8,128]{4,3,2,1,0:T(8,128)(2,1)} %get-tuple-element.33, bf16[2,512,1,8,128]{4,3,2,1,0:T(8,128)(2,1)} %get-tuple-element.31), kind=kOutput, calls=%fused_computation.106 | convolution fusion | flops 1073741824 | bytes 20971520 | tf_op jit(solution)/shard_map/iqhd,ikhd->ihqk/dot_general | solution.py:147
  212.6 18.9 %fusion.100 = (f32[2,8,512]{2,1,0:T(8,128)S(1)}, f32[2,8,512,512]{2,3,1,0:T(8,128)}) fusion(f32[2,8,512,512]{2,3,1,0:T(8,128)} %fusion.52), kind=kOutput, calls=%fused_computation.208 | output fusion | flops 16777728 | bytes 33587200 | tf_op jit(solution)/shard_map/sub | solution.py:149
  231.6 8.4 %convert_bitcast_fusion.2 = bf16[2,512,8,128]{1,3,2,0:T(8,128)(2,1)} fusion(bf16[2,512,1,8,128]{1,4,3,0,2:T(8,128)(2,1)S(1)} %copy-done.22, f32[2,8,512,512]{2,3,1,0:T(8,128)} %get-tuple-element.74, f32[2,8,512]{2,1,0:T(8,128)S(1)} %get-tuple-element.73), kind=kOutput, calls=%fused_computation.105 | convolution fusion | flops 1083179008 | bytes 21004288 | tf_op jit(solution)/shard_map/ihqk,ikhd->iqhd/dot_general | solution.py:152
  244.3 4.9 fusion.101
  252.3 5.9 convert_reduce_fusion.2
  258.2 4.6 fusion.91
  262.9 4.7 fusion.92
  277.1 4.4 fusion.41
  287.8 10.7 %fusion.38 = bf16[2,512,1,8,128]{1,4,3,0,2:T(8,128)(2,1)} fusion(bf16[2,512,8,128]{1,3,2,0:T(8,128)(2,1)} %copy.53, f32[2,8,512,512]{2,3,1,0:T(8,128)} %get-tuple-element.74, f32[2,8,512]{2,1,0:T(8,128)S(1)} %get-tuple-element.73), kind=kOutput, calls=%fused_computation.94 | convolution fusion | flops 1082130432 | bytes 21004288 | tf_op jit(solution)/shard_map/ihqk,iqhd->ikhd/dot_general | solution.py:172
  298.5 10.9 %multiply_reduce_fusion = (f32[2,8,512]{2,1,0:T(8,128)S(1)}, f32[2,8,512,512]{2,3,1,0:T(8,128)}) fusion(f32[2,8,512,512]{2,3,1,0:T(8,128)} %get-tuple-element.74, f32[2,8,512]{2,1,0:T(8,128)S(1)} %get-tuple-element.73, bf16[2,512,8,128]{1,3,2,0:T(8,128)(2,1)S(1)} %copy-done.25, bf16[2,512,1,8,128]{1,4,3,0,2:T(8,128)(2,1)S(1)} %copy-done.23), kind=kOutput, calls=%fused_computation.2 | convolution fusion | flops 1086316544 | bytes 37814272 | tf_op jit(solution)/shard_map/iqhd,ikhd->ihqk/dot_general | solution.py:173
  309.4 11.9 %multiply_convert_fusion = bf16[2,8,512,512]{2,3,1,0:T(8,128)(2,1)S(1)} fusion(f32[2,8,512,512]{2,3,1,0:T(8,128)} %get-tuple-element.79, f32[2,8,512]{2,1,0:T(8,128)S(1)} %get-tuple-element.78, f32[2,8,512,512]{2,3,1,0:T(8,128)} %get-tuple-element.74, f32[2,8,512]{2,1,0:T(8,128)S(1)} %get-tuple-element.73), kind=kLoop, calls=%fused_computation.1 | loop fusion | flops 16777216 | bytes 42008576 | tf_op jit(solution)/shard_map/convert_element_type | solution.py:174
  330.9 5.7 pad_maximum_fusion
  336.7 16.9 %reshape.232 = f32[4,2,128,2,2,768]{2,1,0,5,4,3:T(2,128)} reshape(f32[1024,3072]{0,1:T(8,128)} %pad_maximum_fusion) | data formatting | bytes 25165824 | tf_op jit(solution)/shard_map/reshape | solution.py:84
  353.6 6.6 %constant_dynamic-slice_fusion.1 = bf16[4,2,128,1,2,768]{2,1,0,5,4,3:T(2,128)(2,1)} fusion(f32[4,2,128,2,2,768]{2,1,0,5,4,3:T(2,128)} %reshape.232, s32[]{:T(128)S(6)} %select_n.250), kind=kLoop, calls=%fused_computation.178 | loop fusion | bytes 6291460 | tf_op jit(solution)/shard_map/jit(dynamic_index_in_dim)/dynamic_slice | solution.py:87
  360.1 8.7 %copy.89 = bf16[4,2,128,1,2,768]{5,2,0,1,4,3:T(8,128)(2,1)} copy(bf16[4,2,128,1,2,768]{2,1,0,5,4,3:T(2,128)(2,1)} %constant_dynamic-slice_fusion.1) | data formatting | bytes 6291456
  369.2 6.1 convert_reduce_fusion
  375.3 9.2 %copy.55 = bf16[2,512,3,8,128]{4,3,2,1,0:T(8,128)(2,1)} copy(bf16[2,512,3,8,128]{1,4,3,0,2:T(8,128)(2,1)} %get-tuple-element.28) | data formatting | bytes 12582912 | tf_op jit(solution)/shard_map/convert_element_type | solution.py:177
  384.5 10.3 %convert_element_type.247 = bf16[1024,3072]{1,0:T(8,128)(2,1)} reshape(bf16[2,512,3,8,128]{4,3,2,1,0:T(8,128)(2,1)} %copy.55) | data formatting | bytes 12582912 | tf_op jit(solution)/shard_map/convert_element_type | solution.py:177
  394.8 12.4 %fusion.93 = (f32[1024]{0:T(1024)S(1)}, f32[1024]{0:T(1024)S(1)}, f32[1024,1024]{1,0:T(8,128)}) fusion(f32[1024]{0:T(1024)S(1)} %bitcast.371, f32[1024]{0:T(1024)S(1)} %bitcast.376, bf16[1,2,512,1024]{3,2,1,0:T(8,128)(2,1)S(1)} %copy-done.2, bf16[1024,3072]{1,0:T(8,128)(2,1)} %convert_element_type.247, bf16[1024,3072]{1,0:T(8,128)(2,1)} %bitcast.344), kind=kOutput, calls=%fused_computation.202 | convolution fusion | flops 6448740352 | bytes 18890752 | tf_op jit(solution)/shard_map/dot_general | solution.py:139
  407.2 8.9 %copy.56 = bf16[3072,1024]{1,0:T(8,128)(2,1)} copy(bf16[3072,1024]{0,1:T(8,128)(2,1)} %bitcast.325) | data formatting | bytes 12582912 | tf_op jit(solution)/shard_map/dot_general | solution.py:139
  416.1 5.1 fusion.25
  425.2 9.5 %fusion.102 = f32[4,2,128,2,2,768]{5,2,4,3,1,0:T(8,128)S(1)} fusion(bf16[4,2,128,1024,1,1]{3,2,5,4,1,0:T(8,128)(2,1)} %bitcast.352, bf16[2,2,768,1024,1,1]{3,2,1,0,5,4:T(8,128)(2,1)} %bitcast.345), kind=kOutput, calls=%fused_computation.210 | convolution fusion | flops 6442450944 | bytes 20971520 | tf_op jit(solution)/shard_map/dot_general | solution.py:139
  434.7 4.5 copy-done.15
  443.4 7.6 %constant_dynamic-slice_fusion.2 = f32[4,2,128,1,2,768]{2,1,0,5,4,3:T(2,128)} fusion(f32[4,2,128,2,2,768]{2,1,0,5,4,3:T(2,128)} %reshape.232, s32[]{:T(128)S(6)} %select_n.249), kind=kLoop, calls=%fused_computation.179 | loop fusion | bytes 12582916 | tf_op jit(solution)/shard_map/dynamic-slice.2
  451.0 10.5 %copy.88 = f32[4,2,128,1,2,768]{5,2,0,1,4,3:T(8,128)} copy(f32[4,2,128,1,2,768]{2,1,0,5,4,3:T(2,128)} %constant_dynamic-slice_fusion.2) | data formatting | bytes 12582912
  462.9 4.4 bitcast_add_fusion.1
  469.4 4.5 bitcast_add_fusion
  480.5 8.5 %add_convert_fusion.2 = bf16[1024,1024]{1,0:T(8,128)(2,1)} fusion(f32[1024,1024]{1,0:T(8,128)} %copy-done.10, f32[1024]{0:T(1024)S(1)} %bitcast.394, bf16[1024,3072]{1,0:T(8,128)(2,1)} %bitcast.336, f32[1024,1024]{1,0:T(8,128)} %copy-done.42, f32[1024]{0:T(1024)S(1)} %bitcast.393), kind=kOutput, calls=%fused_computation.75 | convolution fusion | flops 2161115136 | bytes 12591104 | tf_op jit(solution)/shard_map/dot_general | solution.py:139
  491.5 22.9 %collective-permute-done.21 = bf16[2,4,128,768]{3,2,0,1:T(8,128)(2,1)S(1)} collective-permute-done((bf16[2,4,128,768]{3,2,0,1:T(8,128)(2,1)S(1)}, bf16[2,4,128,768]{3,2,0,1:T(8,128)(2,1)S(1)}, u32[]{:S(2)}, u32[]{:S(2)}) %collective-permute-start.21) | collective-permute-done | bytes 1572896 | tf_op jit(solution)/shard_map/ppermute | solution.py:47
  520.9 58.8 %all-reduce.2.cloned.1.call-done = f32[16,1024]{1,0:T(8,128)} async-done(((f32[16,1024]{1,0:T(8,128)}), f32[16,1024]{1,0:T(8,128)}) %all-reduce.2.cloned.1.call-update) | async-done | bytes 65552 | tf_op jit(solution)/shard_map/psum | solution.py:187
  600.3 16.3 %collective-permute-done.33 = bf16[128,768]{1,0:T(8,128)(2,1)S(1)} collective-permute-done((bf16[128,768]{1,0:T(8,128)(2,1)S(1)}, bf16[128,768]{1,0:T(8,128)(2,1)S(1)}, u32[]{:S(2)}, u32[]{:S(2)}) %collective-permute-start.33) | collective-permute-done | bytes 196640 | tf_op jit(solution)/shard_map/ppermute | solution.py:47
  618.9 5.7 collective-permute-done.24
  (263 shorter events, 154.2 us)
Async XLA Ops:
  7.2 572.5 %all-reduce.2.cloned.1.call-start = ((), (), s32[]{:S(2)}) async-start(), calls=%async_computation | async-start | bytes 131072 | tf_op jit(solution)/shard_map/psum | solution.py:187
  8.3 59.0 %collective-permute-start.2 = (bf16[32,3072]{1,0:T(8,128)(2,1)S(1)}, bf16[32,3072]{1,0:T(8,128)(2,1)S(1)}, u32[]{:S(2)}, u32[]{:S(2)}) collective-permute-start(bf16[32,3072]{1,0:T(8,128)(2,1)S(1)} %fusion.119), channel_id=1, source_target_pairs={{0,24},{1,25},{2,26},{3,27},{4,28},{5,29},{6,30},{7,31},{8,16},{9,... | collective-permute-start | bytes 589832 | tf_op jit(solution)/shard_map/ppermute | solution.py:47
  13.4 54.2 %collective-permute-start.1 = (bf16[32,3072]{1,0:T(8,128)(2,1)S(1)}, bf16[32,3072]{1,0:T(8,128)(2,1)S(1)}, u32[]{:S(2)}, u32[]{:S(2)}) collective-permute-start(bf16[32,3072]{1,0:T(8,128)(2,1)S(1)} %fusion.119), channel_id=1, source_target_pairs={{0,16},{1,17},{2,18},{3,19},{4,20},{5,21},{6,22},{7,23},{8,24},{9,... | collective-permute-start | bytes 589832 | tf_op jit(solution)/shard_map/ppermute | solution.py:47
  13.5 54.2 %collective-permute-start = (bf16[32,3072]{1,0:T(8,128)(2,1)S(1)}, bf16[32,3072]{1,0:T(8,128)(2,1)S(1)}, u32[]{:S(2)}, u32[]{:S(2)}) collective-permute-start(bf16[32,3072]{1,0:T(8,128)(2,1)S(1)} %fusion.119), channel_id=1, source_target_pairs={{0,8},{1,9},{2,10},{3,11},{4,12},{5,13},{6,14},{7,15},{8,0},{9,1},... | collective-permute-start | bytes 589832 | tf_op jit(solution)/shard_map/ppermute | solution.py:47
  16.0 57.5 %collective-permute-start.12 = (bf16[32,3072]{1,0:T(8,128)(2,1)}, bf16[32,3072]{1,0:T(8,128)(2,1)S(1)}, u32[]{:S(2)}, u32[]{:S(2)}) collective-permute-start(bf16[32,3072]{1,0:T(8,128)(2,1)} %fusion.120), channel_id=1, source_target_pairs={{0,24},{1,25},{2,26},{3,27},{4,28},{5,29},{6,30},{7,31},{8,16},{9,... | collective-permute-start | bytes 589832 | tf_op jit(solution)/shard_map/ppermute | solution.py:47
  19.7 53.9 %collective-permute-start.11 = (bf16[32,3072]{1,0:T(8,128)(2,1)}, bf16[32,3072]{1,0:T(8,128)(2,1)S(1)}, u32[]{:S(2)}, u32[]{:S(2)}) collective-permute-start(bf16[32,3072]{1,0:T(8,128)(2,1)} %fusion.120), channel_id=1, source_target_pairs={{0,16},{1,17},{2,18},{3,19},{4,20},{5,21},{6,22},{7,23},{8,24},{9,... | collective-permute-start | bytes 589832 | tf_op jit(solution)/shard_map/ppermute | solution.py:47
  67.3 190.9 %copy-start.34 = (f32[1,1024]{1,0:T(1,128)}, f32[1,1024]{1,0:T(1,128)S(1)}, u32[]{:S(2)}) copy-start(f32[1,1024]{1,0:T(1,128)S(1)} %get-tuple-element.56) | copy-start | bytes 12292
  67.3 6.3 collective-permute-start.10
  68.6 16.0 %collective-permute-start.4 = (bf16[4,32,3072]{2,1,0:T(8,128)(2,1)}, bf16[4,32,3072]{2,1,0:T(8,128)(2,1)}, u32[]{:S(2)}, u32[]{:S(2)}) collective-permute-start(bf16[4,32,3072]{2,1,0:T(8,128)(2,1)} %get-tuple-element.53), channel_id=1, source_target_pairs={{0,2},{1,5},{2,0},{3,7},{4,6},{5,1},{6,4},{7,3},{8,10},{9,13},{10,... | collective-permute-start | bytes 2359304 | tf_op jit(solution)/shard_map/ppermute | solution.py:47
  70.1 17.6 %collective-permute-start.3 = (bf16[4,32,3072]{2,1,0:T(8,128)(2,1)}, bf16[4,32,3072]{2,1,0:T(8,128)(2,1)}, u32[]{:S(2)}, u32[]{:S(2)}) collective-permute-start(bf16[4,32,3072]{2,1,0:T(8,128)(2,1)} %get-tuple-element.53), channel_id=1, source_target_pairs={{0,4},{1,3},{2,6},{3,1},{4,0},{5,7},{6,2},{7,5},{8,12},{9,11},{10,... | collective-permute-start | bytes 2359304 | tf_op jit(solution)/shard_map/ppermute | solution.py:47
  73.5 48.8 %collective-permute-start.6 = (bf16[4,32,3072]{2,1,0:T(8,128)(2,1)}, bf16[4,32,3072]{2,1,0:T(8,128)(2,1)S(1)}, u32[]{:S(2)}, u32[]{:S(2)}) collective-permute-start(bf16[4,32,3072]{2,1,0:T(8,128)(2,1)} %get-tuple-element.53), channel_id=1, source_target_pairs={{0,1},{1,0},{2,3},{3,2},{4,5},{5,4},{6,7},{7,6},{8,9},{9,8},{10,11... | collective-permute-start | bytes 2359304 | tf_op jit(solution)/shard_map/ppermute | solution.py:47
  74.7 26.7 %collective-permute-start.14 = (bf16[4,32,3072]{2,1,0:T(8,128)(2,1)S(1)}, bf16[4,32,3072]{2,1,0:T(8,128)(2,1)S(1)}, u32[]{:S(2)}, u32[]{:S(2)}) collective-permute-start(bf16[4,32,3072]{2,1,0:T(8,128)(2,1)S(1)} %get-tuple-element.55), channel_id=1, source_target_pairs={{0,2},{1,5},{2,0},{3,7},{4,6},{5,1},{6,4},{7,3},{8,10},{9,13},{10,... | collective-permute-start | bytes 2359304 | tf_op jit(solution)/shard_map/ppermute | solution.py:47
  76.0 25.4 %collective-permute-start.13 = (bf16[4,32,3072]{2,1,0:T(8,128)(2,1)S(1)}, bf16[4,32,3072]{2,1,0:T(8,128)(2,1)S(1)}, u32[]{:S(2)}, u32[]{:S(2)}) collective-permute-start(bf16[4,32,3072]{2,1,0:T(8,128)(2,1)S(1)} %get-tuple-element.55), channel_id=1, source_target_pairs={{0,4},{1,3},{2,6},{3,1},{4,0},{5,7},{6,2},{7,5},{8,12},{9,11},{10,... | collective-permute-start | bytes 2359304 | tf_op jit(solution)/shard_map/ppermute | solution.py:47
  84.6 23.0 %collective-permute-start.5 = (bf16[4,32,3072]{2,1,0:T(8,128)(2,1)}, bf16[4,32,3072]{2,1,0:T(8,128)(2,1)S(1)}, u32[]{:S(2)}, u32[]{:S(2)}) collective-permute-start(bf16[4,32,3072]{2,1,0:T(8,128)(2,1)} %collective-permute-done.4), channel_id=1, source_target_pairs={{0,4},{1,3},{2,6},{3,1},{4,0},{5,7},{6,2},{7,5},{8,12},{9,11},{10,... | collective-permute-start | bytes 2359304 | tf_op jit(solution)/shard_map/ppermute | solution.py:47
  87.7 29.7 %collective-permute-start.8 = (bf16[4,32,3072]{2,1,0:T(8,128)(2,1)}, bf16[4,32,3072]{2,1,0:T(8,128)(2,1)S(1)}, u32[]{:S(2)}, u32[]{:S(2)}) collective-permute-start(bf16[4,32,3072]{2,1,0:T(8,128)(2,1)} %collective-permute-done.4), channel_id=1, source_target_pairs={{0,1},{1,0},{2,3},{3,2},{4,5},{5,4},{6,7},{7,6},{8,9},{9,8},{10,11... | collective-permute-start | bytes 2359304 | tf_op jit(solution)/shard_map/ppermute | solution.py:47
  101.4 16.6 %collective-permute-start.7 = (bf16[4,32,3072]{2,1,0:T(8,128)(2,1)}, bf16[4,32,3072]{2,1,0:T(8,128)(2,1)S(1)}, u32[]{:S(2)}, u32[]{:S(2)}) collective-permute-start(bf16[4,32,3072]{2,1,0:T(8,128)(2,1)} %collective-permute-done.3), channel_id=1, source_target_pairs={{0,1},{1,0},{2,3},{3,2},{4,5},{5,4},{6,7},{7,6},{8,9},{9,8},{10,11... | collective-permute-start | bytes 2359304 | tf_op jit(solution)/shard_map/ppermute | solution.py:47
  101.4 14.8 %collective-permute-start.15 = (bf16[4,32,3072]{2,1,0:T(8,128)(2,1)S(1)}, bf16[4,32,3072]{2,1,0:T(8,128)(2,1)}, u32[]{:S(2)}, u32[]{:S(2)}) collective-permute-start(bf16[4,32,3072]{2,1,0:T(8,128)(2,1)S(1)} %collective-permute-done.14), channel_id=1, source_target_pairs={{0,4},{1,3},{2,6},{3,1},{4,0},{5,7},{6,2},{7,5},{8,12},{9,11},{10,... | collective-permute-start | bytes 2359304 | tf_op jit(solution)/shard_map/ppermute | solution.py:47
  107.6 10.6 %collective-permute-start.18 = (bf16[4,32,3072]{2,1,0:T(8,128)(2,1)S(1)}, bf16[4,32,3072]{2,1,0:T(8,128)(2,1)S(1)}, u32[]{:S(2)}, u32[]{:S(2)}) collective-permute-start(bf16[4,32,3072]{2,1,0:T(8,128)(2,1)S(1)} %collective-permute-done.14), channel_id=1, source_target_pairs={{0,1},{1,0},{2,3},{3,2},{4,5},{5,4},{6,7},{7,6},{8,9},{9,8},{10,11... | collective-permute-start | bytes 2359304 | tf_op jit(solution)/shard_map/ppermute | solution.py:47
  116.2 2.6 collective-permute-start.17
  117.5 2.5 collective-permute-start.16
  118.0 4.2 collective-permute-start.9
  118.2 6.9 %collective-permute-start.19 = (bf16[4,32,3072]{2,1,0:T(8,128)(2,1)}, bf16[4,32,3072]{2,1,0:T(8,128)(2,1)}, u32[]{:S(2)}, u32[]{:S(2)}) collective-permute-start(bf16[4,32,3072]{2,1,0:T(8,128)(2,1)} %collective-permute-done.15), channel_id=1, source_target_pairs={{0,1},{1,0},{2,3},{3,2},{4,5},{5,4},{6,7},{7,6},{8,9},{9,8},{10,11... | collective-permute-start | bytes 2359304 | tf_op jit(solution)/shard_map/ppermute | solution.py:47
  212.6 18.9 %copy-start.22 = (bf16[2,512,1,8,128]{1,4,3,0,2:T(8,128)(2,1)S(1)}, bf16[2,512,1,8,128]{1,4,3,0,2:T(8,128)(2,1)}, u32[]{:S(2)}) copy-start(bf16[2,512,1,8,128]{1,4,3,0,2:T(8,128)(2,1)} %copy.84) | copy-start | bytes 6291460
  249.2 21.4 %copy-start.10 = (f32[1024,1024]{1,0:T(8,128)}, f32[1024,1024]{1,0:T(8,128)S(1)}, u32[]{:S(2)}) copy-start(f32[1024,1024]{1,0:T(8,128)S(1)} %get-tuple-element.76) | copy-start | bytes 12582916
  368.8 94.1 %collective-permute-start.29 = (bf16[2,2,4,128,768]{4,3,2,0,1:T(8,128)(2,1)}, bf16[2,2,4,128,768]{4,3,2,0,1:T(8,128)(2,1)}, u32[]{:S(2)}, u32[]{:S(2)}) collective-permute-start(bf16[2,2,4,128,768]{4,3,2,0,1:T(8,128)(2,1)} %bitcast.348), channel_id=1, source_target_pairs={{0,1},{1,0},{2,3},{3,2},{4,5},{5,4},{6,7},{7,6},{8,9},{9,8},{10,11... | collective-permute-start | bytes 9437192 | tf_op jit(solution)/shard_map/ppermute | solution.py:47
  441.3 28.1 %collective-permute-start.20 = (bf16[2,2,4,128,768]{4,3,1,0,2:T(8,128)(2,1)}, bf16[2,2,4,128,768]{4,3,1,0,2:T(8,128)(2,1)}, u32[]{:S(2)}, u32[]{:S(2)}) collective-permute-start(bf16[2,2,4,128,768]{4,3,1,0,2:T(8,128)(2,1)} %fusion.36), channel_id=1, source_target_pairs={{0,1},{1,0},{2,3},{3,2},{4,5},{5,4},{6,7},{7,6},{8,9},{9,8},{10,11... | collective-permute-start | bytes 9437192 | tf_op jit(solution)/shard_map/ppermute | solution.py:47
  468.2 20.8 %collective-permute-start.30 = (bf16[2,4,128,768]{3,2,1,0:T(8,128)(2,1)S(1)}, bf16[2,4,128,768]{3,2,1,0:T(8,128)(2,1)S(1)}, u32[]{:S(2)}, u32[]{:S(2)}) collective-permute-start(bf16[2,4,128,768]{3,2,1,0:T(8,128)(2,1)S(1)} %fusion.68), channel_id=1, source_target_pairs={{0,4},{1,3},{2,6},{3,1},{4,0},{5,7},{6,2},{7,5},{8,12},{9,11},{10,... | collective-permute-start | bytes 4718600 | tf_op jit(solution)/shard_map/ppermute | solution.py:47
  477.3 37.2 %slice-start = ((s8[6291456]{0:T(1024)(128)(4,1)}), s8[4194304]{0:T(1024)(128)(4,1)S(1)}, s32[]{:S(2)}) async-start(s8[6291456]{0:T(1024)(128)(4,1)} %bitcast.329), calls=%async_computation.1 | async-start | bytes 8388608
  479.5 34.9 %collective-permute-start.21 = (bf16[2,4,128,768]{3,2,0,1:T(8,128)(2,1)S(1)}, bf16[2,4,128,768]{3,2,0,1:T(8,128)(2,1)S(1)}, u32[]{:S(2)}, u32[]{:S(2)}) collective-permute-start(bf16[2,4,128,768]{3,2,0,1:T(8,128)(2,1)S(1)} %fusion.67), channel_id=1, source_target_pairs={{0,4},{1,3},{2,6},{3,1},{4,0},{5,7},{6,2},{7,5},{8,12},{9,11},{10,... | collective-permute-start | bytes 4718600 | tf_op jit(solution)/shard_map/ppermute | solution.py:47
  480.5 34.0 %slice-start.1 = ((s8[6291456]{0:T(1024)(128)(4,1)}), s8[2097152]{0:T(1024)(128)(4,1)S(1)}, s32[]{:S(2)}) async-start(s8[6291456]{0:T(1024)(128)(4,1)} %bitcast.329), calls=%async_computation.2 | async-start | bytes 4194304
  489.3 28.5 %copy-start.11 = (f32[1024,1024]{1,0:T(8,128)S(1)}, f32[1024,1024]{1,0:T(8,128)}, u32[]{:S(2)}) copy-start(f32[1024,1024]{1,0:T(8,128)} %get-tuple-element.80) | copy-start | bytes 12582916
  490.3 27.6 %copy-start.4 = (f32[1024,1024]{1,0:T(8,128)S(1)}, f32[1024,1024]{1,0:T(8,128)}, u32[]{:S(2)}) copy-start(f32[1024,1024]{1,0:T(8,128)} %copy-done.3) | copy-start | bytes 12582916
  490.3 27.6 %copy-start.8 = (bf16[1,2,512,1024]{3,2,1,0:T(8,128)(2,1)S(1)}, bf16[1,2,512,1024]{3,2,1,0:T(8,128)(2,1)}, u32[]{:S(2)}) copy-start(bf16[1,2,512,1024]{3,2,1,0:T(8,128)(2,1)} %param.17) | copy-start | bytes 6291460
  490.3 27.6 %copy-start.31 = (f32[1024]{0:T(1024)S(1)}, f32[1024]{0:T(1024)}, u32[]{:S(2)}) copy-start(f32[1024]{0:T(1024)} %copy-done.30) | copy-start | bytes 12292
  490.3 93.4 %collective-permute-start.31 = (bf16[4,128,768]{2,1,0:T(8,128)(2,1)}, bf16[4,128,768]{2,1,0:T(8,128)(2,1)}, u32[]{:S(2)}, u32[]{:S(2)}) collective-permute-start(bf16[4,128,768]{2,1,0:T(8,128)(2,1)} %fusion.70), channel_id=1, source_target_pairs={{0,2},{1,5},{2,0},{3,7},{4,6},{5,1},{6,4},{7,3},{8,10},{9,13},{10,... | collective-permute-start | bytes 2359304 | tf_op jit(solution)/shard_map/ppermute | solution.py:47
  516.5 73.6 %collective-permute-start.22 = (bf16[4,128,768]{2,1,0:T(8,128)(2,1)S(1)}, bf16[4,128,768]{2,1,0:T(8,128)(2,1)}, u32[]{:S(2)}, u32[]{:S(2)}) collective-permute-start(bf16[4,128,768]{2,1,0:T(8,128)(2,1)S(1)} %fusion.69), channel_id=1, source_target_pairs={{0,2},{1,5},{2,0},{3,7},{4,6},{5,1},{6,4},{7,3},{8,10},{9,13},{10,... | collective-permute-start | bytes 2359304 | tf_op jit(solution)/shard_map/ppermute | solution.py:47
  585.5 10.5 %collective-permute-start.32 = (bf16[128,768]{1,0:T(8,128)(2,1)S(1)}, bf16[128,768]{1,0:T(8,128)(2,1)S(1)}, u32[]{:S(2)}, u32[]{:S(2)}) collective-permute-start(bf16[128,768]{1,0:T(8,128)(2,1)S(1)} %get-tuple-element.38), channel_id=1, source_target_pairs={{0,8},{1,9},{2,10},{3,11},{4,12},{5,13},{6,14},{7,15},{8,0},{9,1},... | collective-permute-start | bytes 589832 | tf_op jit(solution)/shard_map/ppermute | solution.py:47
  588.3 11.9 %collective-permute-start.34 = (bf16[128,768]{1,0:T(8,128)(2,1)S(1)}, bf16[128,768]{1,0:T(8,128)(2,1)S(1)}, u32[]{:S(2)}, u32[]{:S(2)}) collective-permute-start(bf16[128,768]{1,0:T(8,128)(2,1)S(1)} %get-tuple-element.39), channel_id=1, source_target_pairs={{0,24},{1,25},{2,26},{3,27},{4,28},{5,29},{6,30},{7,31},{8,16},{9,... | collective-permute-start | bytes 589832 | tf_op jit(solution)/shard_map/ppermute | solution.py:47
  590.1 26.5 %collective-permute-start.33 = (bf16[128,768]{1,0:T(8,128)(2,1)S(1)}, bf16[128,768]{1,0:T(8,128)(2,1)S(1)}, u32[]{:S(2)}, u32[]{:S(2)}) collective-permute-start(bf16[128,768]{1,0:T(8,128)(2,1)S(1)} %get-tuple-element.40), channel_id=1, source_target_pairs={{0,16},{1,17},{2,18},{3,19},{4,20},{5,21},{6,22},{7,23},{8,24},{9,... | collective-permute-start | bytes 589832 | tf_op jit(solution)/shard_map/ppermute | solution.py:47
  591.6 26.8 %collective-permute-start.23 = (bf16[128,768]{1,0:T(8,128)(2,1)S(1)}, bf16[128,768]{1,0:T(8,128)(2,1)S(1)}, u32[]{:S(2)}, u32[]{:S(2)}) collective-permute-start(bf16[128,768]{1,0:T(8,128)(2,1)S(1)} %get-tuple-element.41), channel_id=1, source_target_pairs={{0,8},{1,9},{2,10},{3,11},{4,12},{5,13},{6,14},{7,15},{8,0},{9,1},... | collective-permute-start | bytes 589832 | tf_op jit(solution)/shard_map/ppermute | solution.py:47
  594.2 24.7 %collective-permute-start.25 = (bf16[128,768]{1,0:T(8,128)(2,1)S(1)}, bf16[128,768]{1,0:T(8,128)(2,1)S(1)}, u32[]{:S(2)}, u32[]{:S(2)}) collective-permute-start(bf16[128,768]{1,0:T(8,128)(2,1)S(1)} %get-tuple-element.42), channel_id=1, source_target_pairs={{0,24},{1,25},{2,26},{3,27},{4,28},{5,29},{6,30},{7,31},{8,16},{9,... | collective-permute-start | bytes 589832 | tf_op jit(solution)/shard_map/ppermute | solution.py:47
  596.0 28.6 %collective-permute-start.24 = (bf16[128,768]{1,0:T(8,128)(2,1)S(1)}, bf16[128,768]{1,0:T(8,128)(2,1)S(1)}, u32[]{:S(2)}, u32[]{:S(2)}) collective-permute-start(bf16[128,768]{1,0:T(8,128)(2,1)S(1)} %get-tuple-element.43), channel_id=1, source_target_pairs={{0,16},{1,17},{2,18},{3,19},{4,20},{5,21},{6,22},{7,23},{8,24},{9,... | collective-permute-start | bytes 589832 | tf_op jit(solution)/shard_map/ppermute | solution.py:47
  616.7 9.7 %collective-permute-start.37 = (bf16[128,768]{1,0:T(8,128)(2,1)S(1)}, bf16[128,768]{1,0:T(8,128)(2,1)S(1)}, u32[]{:S(2)}, u32[]{:S(2)}) collective-permute-start(bf16[128,768]{1,0:T(8,128)(2,1)S(1)} %fusion.73), channel_id=1, source_target_pairs={{0,3},{1,2},{2,1},{3,0},{4,7},{5,6},{6,5},{7,4},{8,11},{9,10},{10,... | collective-permute-start | bytes 589832 | tf_op jit(solution)/shard_map/ppermute | solution.py:47
  617.2 9.8 %collective-permute-start.36 = (bf16[128,768]{1,0:T(8,128)(2,1)S(1)}, bf16[128,768]{1,0:T(8,128)(2,1)S(1)}, u32[]{:S(2)}, u32[]{:S(2)}) collective-permute-start(bf16[128,768]{1,0:T(8,128)(2,1)S(1)} %fusion.73), channel_id=1, source_target_pairs={{0,1},{1,0},{2,3},{3,2},{4,5},{5,4},{6,7},{7,6},{8,9},{9,8},{10,11... | collective-permute-start | bytes 589832 | tf_op jit(solution)/shard_map/ppermute | solution.py:47
  618.4 9.8 %collective-permute-start.35 = (bf16[128,768]{1,0:T(8,128)(2,1)S(1)}, bf16[128,768]{1,0:T(8,128)(2,1)S(1)}, u32[]{:S(2)}, u32[]{:S(2)}) collective-permute-start(bf16[128,768]{1,0:T(8,128)(2,1)S(1)} %fusion.73), channel_id=1, source_target_pairs={{0,2},{1,3},{2,0},{3,1},{4,6},{5,7},{6,4},{7,5},{8,10},{9,11},{10,... | collective-permute-start | bytes 589832 | tf_op jit(solution)/shard_map/ppermute | solution.py:47
  624.8 10.0 %collective-permute-start.28 = (bf16[128,768]{1,0:T(8,128)(2,1)S(1)}, bf16[128,768]{1,0:T(8,128)(2,1)}, u32[]{:S(2)}, u32[]{:S(2)}) collective-permute-start(bf16[128,768]{1,0:T(8,128)(2,1)S(1)} %fusion.76), channel_id=1, source_target_pairs={{0,3},{1,2},{2,1},{3,0},{4,7},{5,6},{6,5},{7,4},{8,11},{9,10},{10,... | collective-permute-start | bytes 589832 | tf_op jit(solution)/shard_map/ppermute | solution.py:47
  625.6 9.1 %collective-permute-start.27 = (bf16[128,768]{1,0:T(8,128)(2,1)S(1)}, bf16[128,768]{1,0:T(8,128)(2,1)}, u32[]{:S(2)}, u32[]{:S(2)}) collective-permute-start(bf16[128,768]{1,0:T(8,128)(2,1)S(1)} %fusion.76), channel_id=1, source_target_pairs={{0,1},{1,0},{2,3},{3,2},{4,5},{5,4},{6,7},{7,6},{8,9},{9,8},{10,11... | collective-permute-start | bytes 589832 | tf_op jit(solution)/shard_map/ppermute | solution.py:47
  626.4 10.3 %collective-permute-start.26 = (bf16[128,768]{1,0:T(8,128)(2,1)S(1)}, bf16[128,768]{1,0:T(8,128)(2,1)}, u32[]{:S(2)}, u32[]{:S(2)}) collective-permute-start(bf16[128,768]{1,0:T(8,128)(2,1)S(1)} %fusion.76), channel_id=1, source_target_pairs={{0,2},{1,3},{2,0},{3,1},{4,6},{5,7},{6,4},{7,5},{8,10},{9,11},{10,... | collective-permute-start | bytes 589832 | tf_op jit(solution)/shard_map/ppermute | solution.py:47
  (38 other events, 245.2 us)
Sparse Core Ops, SparseCore 0:
  463.1 116.6 all-reduce.1
where the time goes:
time: 659 us; the launch traced here: 650 us
  local copies, waits for them, and re-layouts  144 us (22%)
  other arithmetic  143 us (22%)
  waiting for transfers between devices  143 us (22%)
  matrix products  119 us (18%)
  blocking collectives  45.8 us (7%)
  starting transfers between devices  40.6 us (6%)
  between operations  15.4 us (2%)
    ppermute x38, waiting for transfers between devices, move(): return lax.ppermute(value, AXES, pairs)  83.7 us
    dot_general x12, matrix products, dot(): return lax.dot_general(a, b, (dims, ((), ())), preferred_element_type=F32)  71.4 us
    psum x1, waiting for transfers between devices, per_device(): smalls = lax.psum(smalls, AXES)  58.8 us
    unnamed x105, local copies, waits for them, and re-layouts  49.5 us
    select_n x12, other arithmetic, flip_if(): return jnp.where(bit == 1, jnp.flip(value, axis), value)  49 us
    all_gather x1, blocking collectives, per_device(): small = lax.all_gather(small, 'batch', axis=1, tiled=True)  45.8 us
    ppermute x38, starting transfers between devices, move(): return lax.ppermute(value, AXES, pairs)  40.5 us
    convert_element_type x2, local copies, waits for them, and re-layouts, per_device(): jnp.stack([g_q, g_k, g_v], axis=2).astype(BF).reshape(-1, 3 * width)  19.5 us
  transfers between devices with their start and end apart: 39, of which 13 were waited for; matrix products, arithmetic and copies ran while one was open for 23% of the time, Pallas kernels for 0%

commit v1 on v0

--- a/solution.py
+++ b/solution.py
@@ -127,7 +127,16 @@
         )
     else:
         links = Links(nb, nr)
-        small = lax.all_gather(small, "batch", axis=1, tiled=True)
+        ways = lax.axis_size("batch")
+        up = [(d, (d + 1) % ways) for d in range(ways)]
+        down = [(d, (d - 1) % ways) for d in range(ways)]
+        earlier, later = ([small], [small])
+        for _ in range(ways // 2):
+            earlier.append(lax.ppermute(earlier[-1], "batch", up))
+        for _ in range((ways - 1) // 2):
+            later.append(lax.ppermute(later[-1], "batch", down))
+        line = jnp.concatenate([*earlier[::-1], *later[1:]], axis=1)
+        small = jnp.roll(line, (lax.axis_index("batch") - ways // 2) * small.shape[1], axis=1)
         w_qkv = gather_rows(w_qkv, links)
         rest = gather_rows(jnp.concatenate([w_out, w_up, w_down], axis=1), links)
         w_out, w_up, w_down = (rest[:, :width], rest[:, width:-width], rest[:, -width:])

time: 659 us -> 646 us (0.980)
  blocking collectives: 45.8 us -> 0 us
  waiting for transfers between devices: 143 us -> 166 us
  starting transfers between devices: 40.6 us -> 52 us
    all_gather x1 -> x0, blocking collectives: 45.8 us -> none  [per_device(): small = lax.all_gather(small, 'batch', axis=1, tiled=True)]
    ppermute x0 -> x7, waiting for transfers between devices: none -> 18.9 us  [the longest x4 15.4 us: per_device(): earlier.append(lax.ppermute(earlier[-1], 'batch', up))]
    ppermute x0 -> x7, starting transfers between devices: none -> 12.3 us  [the longest x3 10.8 us: per_device(): later.append(lax.ppermute(later[-1], 'batch', down))]
    unnamed x105 -> x118, local copies, waits for them, and re-layouts: 49.5 us -> 48.5 us
  transfers between devices with their start and end apart: 39 -> 46, of which waited for: 13 -> 18; matrix products, arithmetic and copies ran while one was open for 23% -> 23% of each run, Pallas kernels for 0% -> 0%
where the time goes in v1:
time: 646 us; the launch traced here: 637 us
  waiting for transfers between devices  166 us (26%)
  local copies, waits for them, and re-layouts  143 us (22%)
  other arithmetic  142 us (22%)
  matrix products  119 us (18%)
  starting transfers between devices  52 us (8%)
  between operations  15.5 us (2%)
    ppermute x38, waiting for transfers between devices, move(): return lax.ppermute(value, AXES, pairs)  87 us
    dot_general x12, matrix products, dot(): return lax.dot_general(a, b, (dims, ((), ())), preferred_element_type=F32)  71.3 us
    psum x1, waiting for transfers between devices, per_device(): smalls = lax.psum(smalls, AXES)  59.7 us
    select_n x12, other arithmetic, flip_if(): return jnp.where(bit == 1, jnp.flip(value, axis), value)  48.9 us
    unnamed x118, local copies, waits for them, and re-layouts  48.5 us
    ppermute x38, starting transfers between devices, move(): return lax.ppermute(value, AXES, pairs)  39.7 us
    convert_element_type x2, local copies, waits for them, and re-layouts, per_device(): jnp.stack([g_q, g_k, g_v], axis=2).astype(BF).reshape(-1, 3 * width)  19.5 us
    sub x1, other arithmetic, per_device(): raised = jnp.exp(scores - top)  19 us
  transfers between devices with their start and end apart: 46, of which 18 were waited for; matrix products, arithmetic and copies ran while one was open for 23% of the time, Pallas kernels for 0%

profile of v1, /device:TPU:0, one launch (start us, length us, event | category | flops | bytes accessed | tf_op | source)
XLA Modules:
  0.0 637.4 jit_solution(10889397442136362786)
XLA Ops:
  8.1 6.0 collective-permute-start.4
  23.7 9.1 %collective-permute-done.1 = bf16[9,128]{1,0:T(8,128)(2,1)S(1)} collective-permute-done((bf16[9,128]{1,0:T(8,128)(2,1)S(1)}, bf16[9,128]{1,0:T(8,128)(2,1)S(1)}, u32[]{:S(2)}, u32[]{:S(2)}) %collective-permute-start.1) | collective-permute-done | bytes 2336 | tf_op jit(solution)/shard_map/ppermute | solution.py:135
  32.8 4.8 collective-permute-start.5
  40.6 4.8 collective-permute-done.3
  61.4 11.4 %collective-permute-done.11 = bf16[4,32,3072]{2,1,0:T(8,128)(2,1)S(1)} collective-permute-done((bf16[4,32,3072]{2,1,0:T(8,128)(2,1)S(1)}, bf16[4,32,3072]{2,1,0:T(8,128)(2,1)S(1)}, u32[]{:S(2)}, u32[]{:S(2)}) %collective-permute-start.11) | collective-permute-done | bytes 786464 | tf_op jit(solution)/shard_map/ppermute | solution.py:47
  75.1 14.5 %collective-permute-done.21 = bf16[4,32,3072]{2,1,0:T(8,128)(2,1)S(1)} collective-permute-done((bf16[4,32,3072]{2,1,0:T(8,128)(2,1)S(1)}, bf16[4,32,3072]{2,1,0:T(8,128)(2,1)S(1)}, u32[]{:S(2)}, u32[]{:S(2)}) %collective-permute-start.21) | collective-permute-done | bytes 786464 | tf_op jit(solution)/shard_map/ppermute | solution.py:47
  94.7 7.1 %collective-permute-done.22 = bf16[4,32,3072]{2,1,0:T(8,128)(2,1)} collective-permute-done((bf16[4,32,3072]{2,1,0:T(8,128)(2,1)S(1)}, bf16[4,32,3072]{2,1,0:T(8,128)(2,1)}, u32[]{:S(2)}, u32[]{:S(2)}) %collective-permute-start.22) | collective-permute-done | bytes 786464 | tf_op jit(solution)/shard_map/ppermute | solution.py:47
  117.1 7.5 %reverse_select_fusion.4 = bf16[2,2,2,4,32,3072]{5,4,3,2,1,0:T(8,128)(2,1)S(1)} fusion(bf16[2,2,2,4,32,3072]{5,4,3,2,1,0:T(8,128)(2,1)} %pad_maximum_fusion.2, pred[]{:T(512)S(6)} %eq.26), kind=kLoop, calls=%fused_computation.14 | loop fusion | flops 3145728 | bytes 12582913 | tf_op jit(solution)/shard_map/jit(_where)/select_n | solution.py:51
  124.5 4.4 reverse_select_fusion.8
  133.3 7.6 %reverse_select_fusion.7 = bf16[2,2,2,4,32,3072]{5,4,2,0,1,3:T(8,128)(2,1)S(1)} fusion(bf16[2,2,2,4,32,3072]{5,4,2,0,1,3:T(8,128)(2,1)} %reverse_select_fusion.8, pred[]{:T(512)S(6)} %eq.24), kind=kLoop, calls=%fused_computation.17 | loop fusion | flops 3145728 | bytes 12582913 | tf_op jit(solution)/shard_map/jit(_where)/select_n | solution.py:51
  141.0 4.4 reverse_select_fusion.2
  148.6 4.8 reverse_select_fusion.6
  155.3 7.5 %reverse_select_fusion.5 = bf16[2,2,2,2,2,32,3072]{6,5,2,0,1,4,3:T(8,128)(2,1)S(1)} fusion(bf16[2,2,2,2,2,32,3072]{6,5,2,0,1,4,3:T(8,128)(2,1)} %reverse_select_fusion.6, pred[]{:T(512)S(6)} %eq.22), kind=kLoop, calls=%fused_computation.15 | loop fusion | flops 3145728 | bytes 12582913 | tf_op jit(solution)/shard_map/jit(_where)/select_n | solution.py:51
  167.5 8.6 %fusion.5 = bf16[128,8,24,128]{3,1,2,0:T(8,128)(2,1)} fusion(f32[3072]{0:T(1024)S(1)} %pad_maximum_fusion.8, bf16[1024,1024]{1,0:T(8,128)(2,1)S(1)} %bitcast.349, bf16[1024,3072]{1,0:T(8,128)(2,1)S(1)} %bitcast.343), kind=kOutput, calls=%fused_computation.22 | convolution fusion | flops 6448742400 | bytes 14692352 | tf_op jit(solution)/shard_map/dot_general | solution.py:148
  176.1 4.7 copy.92
  183.9 4.6 copy.84
  188.5 10.3 %fusion.52 = f32[2,8,512,512]{2,3,1,0:T(8,128)} fusion(bf16[2,512,1,8,128]{4,3,2,1,0:T(8,128)(2,1)} %get-tuple-element.33, bf16[2,512,1,8,128]{4,3,2,1,0:T(8,128)(2,1)} %get-tuple-element.31), kind=kOutput, calls=%fused_computation.106 | convolution fusion | flops 1073741824 | bytes 20971520 | tf_op jit(solution)/shard_map/iqhd,ikhd->ihqk/dot_general | solution.py:156
  198.8 19.0 %fusion.100 = (f32[2,8,512]{2,1,0:T(8,128)S(1)}, f32[2,8,512,512]{2,3,1,0:T(8,128)}) fusion(f32[2,8,512,512]{2,3,1,0:T(8,128)} %fusion.52), kind=kOutput, calls=%fused_computation.225 | output fusion | flops 16777728 | bytes 33587200 | tf_op jit(solution)/shard_map/sub | solution.py:158
  217.9 8.4 %convert_bitcast_fusion.2 = bf16[2,512,8,128]{1,3,2,0:T(8,128)(2,1)} fusion(bf16[2,512,1,8,128]{1,4,3,0,2:T(8,128)(2,1)S(1)} %copy-done.22, f32[2,8,512,512]{2,3,1,0:T(8,128)} %get-tuple-element.74, f32[2,8,512]{2,1,0:T(8,128)S(1)} %get-tuple-element.73), kind=kOutput, calls=%fused_computation.105 | convolution fusion | flops 1083179008 | bytes 21004288 | tf_op jit(solution)/shard_map/ihqk,ikhd->iqhd/dot_general | solution.py:161
  230.6 4.9 fusion.101
  238.6 5.9 convert_reduce_fusion.2
  244.5 4.7 fusion.91
  249.2 4.7 fusion.92
  263.4 4.4 fusion.41
  274.1 10.7 %fusion.38 = bf16[2,512,1,8,128]{1,4,3,0,2:T(8,128)(2,1)} fusion(bf16[2,512,8,128]{1,3,2,0:T(8,128)(2,1)} %copy.53, f32[2,8,512,512]{2,3,1,0:T(8,128)} %get-tuple-element.74, f32[2,8,512]{2,1,0:T(8,128)S(1)} %get-tuple-element.73), kind=kOutput, calls=%fused_computation.94 | convolution fusion | flops 1082130432 | bytes 21004288 | tf_op jit(solution)/shard_map/ihqk,iqhd->ikhd/dot_general | solution.py:181
  284.9 10.9 %multiply_reduce_fusion = (f32[2,8,512]{2,1,0:T(8,128)S(1)}, f32[2,8,512,512]{2,3,1,0:T(8,128)}) fusion(f32[2,8,512,512]{2,3,1,0:T(8,128)} %get-tuple-element.74, f32[2,8,512]{2,1,0:T(8,128)S(1)} %get-tuple-element.73, bf16[2,512,8,128]{1,3,2,0:T(8,128)(2,1)S(1)} %copy-done.25, bf16[2,512,1,8,128]{1,4,3,0,2:T(8,128)(2,1)S(1)} %copy-done.23), kind=kOutput, calls=%fused_computation.2 | convolution fusion | flops 1086316544 | bytes 37814272 | tf_op jit(solution)/shard_map/iqhd,ikhd->ihqk/dot_general | solution.py:182
  295.8 11.9 %multiply_convert_fusion = bf16[2,8,512,512]{2,3,1,0:T(8,128)(2,1)S(1)} fusion(f32[2,8,512,512]{2,3,1,0:T(8,128)} %get-tuple-element.79, f32[2,8,512]{2,1,0:T(8,128)S(1)} %get-tuple-element.78, f32[2,8,512,512]{2,3,1,0:T(8,128)} %get-tuple-element.74, f32[2,8,512]{2,1,0:T(8,128)S(1)} %get-tuple-element.73), kind=kLoop, calls=%fused_computation.1 | loop fusion | flops 16777216 | bytes 42008576 | tf_op jit(solution)/shard_map/convert_element_type | solution.py:183
  317.3 5.7 pad_maximum_fusion
  323.0 16.9 %reshape.232 = f32[4,2,128,2,2,768]{2,1,0,5,4,3:T(2,128)} reshape(f32[1024,3072]{0,1:T(8,128)} %pad_maximum_fusion) | data formatting | bytes 25165824 | tf_op jit(solution)/shard_map/reshape | solution.py:84
  340.0 6.5 %constant_dynamic-slice_fusion.1 = bf16[4,2,128,1,2,768]{2,1,0,5,4,3:T(2,128)(2,1)} fusion(f32[4,2,128,2,2,768]{2,1,0,5,4,3:T(2,128)} %reshape.232, s32[]{:T(128)S(6)} %select_n.264), kind=kLoop, calls=%fused_computation.195 | loop fusion | bytes 6291460 | tf_op jit(solution)/shard_map/jit(dynamic_index_in_dim)/dynamic_slice | solution.py:87
  346.5 8.7 %copy.89 = bf16[4,2,128,1,2,768]{5,2,0,1,4,3:T(8,128)(2,1)} copy(bf16[4,2,128,1,2,768]{2,1,0,5,4,3:T(2,128)(2,1)} %constant_dynamic-slice_fusion.1) | data formatting | bytes 6291456
  355.3 6.1 convert_reduce_fusion
  361.5 9.2 %copy.55 = bf16[2,512,3,8,128]{4,3,2,1,0:T(8,128)(2,1)} copy(bf16[2,512,3,8,128]{1,4,3,0,2:T(8,128)(2,1)} %get-tuple-element.28) | data formatting | bytes 12582912 | tf_op jit(solution)/shard_map/convert_element_type | solution.py:186
  370.6 10.3 %convert_element_type.247 = bf16[1024,3072]{1,0:T(8,128)(2,1)} reshape(bf16[2,512,3,8,128]{4,3,2,1,0:T(8,128)(2,1)} %copy.55) | data formatting | bytes 12582912 | tf_op jit(solution)/shard_map/convert_element_type | solution.py:186
  381.0 12.3 %fusion.93 = (f32[1024]{0:T(1024)S(1)}, f32[1024]{0:T(1024)S(1)}, f32[1024,1024]{1,0:T(8,128)}) fusion(f32[1024]{0:T(1024)S(1)} %bitcast.370, f32[1024]{0:T(1024)S(1)} %bitcast.375, bf16[1,2,512,1024]{3,2,1,0:T(8,128)(2,1)S(1)} %copy-done.2, bf16[1024,3072]{1,0:T(8,128)(2,1)} %convert_element_type.247, bf16[1024,3072]{1,0:T(8,128)(2,1)} %bitcast.344), kind=kOutput, calls=%fused_computation.219 | convolution fusion | flops 6448740352 | bytes 18890752 | tf_op jit(solution)/shard_map/dot_general | solution.py:148
  393.3 8.9 %copy.56 = bf16[3072,1024]{1,0:T(8,128)(2,1)} copy(bf16[3072,1024]{0,1:T(8,128)(2,1)} %bitcast.325) | data formatting | bytes 12582912 | tf_op jit(solution)/shard_map/dot_general | solution.py:148
  402.2 5.1 fusion.25
  411.3 9.5 %fusion.102 = f32[4,2,128,2,2,768]{5,2,4,3,1,0:T(8,128)S(1)} fusion(bf16[4,2,128,1024,1,1]{3,2,5,4,1,0:T(8,128)(2,1)} %bitcast.352, bf16[2,2,768,1024,1,1]{3,2,1,0,5,4:T(8,128)(2,1)} %bitcast.345), kind=kOutput, calls=%fused_computation.227 | convolution fusion | flops 6442450944 | bytes 20971520 | tf_op jit(solution)/shard_map/dot_general | solution.py:148
  420.8 4.5 copy-done.15
  429.8 7.6 %constant_dynamic-slice_fusion.2 = f32[4,2,128,1,2,768]{2,1,0,5,4,3:T(2,128)} fusion(f32[4,2,128,2,2,768]{2,1,0,5,4,3:T(2,128)} %reshape.232, s32[]{:T(128)S(6)} %select_n.263), kind=kLoop, calls=%fused_computation.196 | loop fusion | bytes 12582916 | tf_op jit(solution)/shard_map/dynamic-slice.2
  437.4 10.5 %copy.88 = f32[4,2,128,1,2,768]{5,2,0,1,4,3:T(8,128)} copy(f32[4,2,128,1,2,768]{2,1,0,5,4,3:T(2,128)} %constant_dynamic-slice_fusion.2) | data formatting | bytes 12582912
  449.3 4.4 bitcast_add_fusion.1
  455.9 4.5 bitcast_add_fusion
  466.8 8.5 %add_convert_fusion.2 = bf16[1024,1024]{1,0:T(8,128)(2,1)} fusion(f32[1024,1024]{1,0:T(8,128)} %copy-done.10, f32[1024]{0:T(1024)S(1)} %bitcast.396, bf16[1024,3072]{1,0:T(8,128)(2,1)} %bitcast.336, f32[1024,1024]{1,0:T(8,128)} %copy-done.42, f32[1024]{0:T(1024)S(1)} %bitcast.395), kind=kOutput, calls=%fused_computation.75 | convolution fusion | flops 2161115136 | bytes 12591104 | tf_op jit(solution)/shard_map/dot_general | solution.py:148
  478.1 22.5 %collective-permute-done.28 = bf16[2,4,128,768]{3,2,0,1:T(8,128)(2,1)S(1)} collective-permute-done((bf16[2,4,128,768]{3,2,0,1:T(8,128)(2,1)S(1)}, bf16[2,4,128,768]{3,2,0,1:T(8,128)(2,1)S(1)}, u32[]{:S(2)}, u32[]{:S(2)}) %collective-permute-start.28) | collective-permute-done | bytes 1572896 | tf_op jit(solution)/shard_map/ppermute | solution.py:47
  507.3 59.7 %all-reduce.2.cloned.1.call-done = f32[16,1024]{1,0:T(8,128)} async-done(((f32[16,1024]{1,0:T(8,128)}), f32[16,1024]{1,0:T(8,128)}) %all-reduce.2.cloned.1.call-update) | async-done | bytes 65552 | tf_op jit(solution)/shard_map/psum | solution.py:196
  587.6 16.4 %collective-permute-done.40 = bf16[128,768]{1,0:T(8,128)(2,1)S(1)} collective-permute-done((bf16[128,768]{1,0:T(8,128)(2,1)S(1)}, bf16[128,768]{1,0:T(8,128)(2,1)S(1)}, u32[]{:S(2)}, u32[]{:S(2)}) %collective-permute-start.40) | collective-permute-done | bytes 196640 | tf_op jit(solution)/shard_map/ppermute | solution.py:47
  606.2 5.7 collective-permute-done.31
  (293 shorter events, 170.6 us)
Async XLA Ops:
  7.2 38.2 %copy-start.33 = (bf16[6,128]{1,0:T(8,128)(2,1)S(1)}, bf16[6,128]{1,0:T(8,128)(2,1)}, u32[]{:S(2)}) copy-start(bf16[6,128]{1,0:T(8,128)(2,1)} %param.15) | copy-start | bytes 4612
  7.2 559.8 %all-reduce.2.cloned.1.call-start = ((), (), s32[]{:S(2)}) async-start(), calls=%async_computation | async-start | bytes 131072 | tf_op jit(solution)/shard_map/psum | solution.py:196
  8.1 24.7 %collective-permute-start.4 = (bf16[9,128]{1,0:T(8,128)(2,1)S(1)}, bf16[9,128]{1,0:T(8,128)(2,1)S(1)}, u32[]{:S(2)}, u32[]{:S(2)}) collective-permute-start(bf16[9,128]{1,0:T(8,128)(2,1)S(1)} %pad_maximum_fusion.9), channel_id=1, source_target_pairs={{0,28},{4,0},{8,4},{12,8},{16,12},{20,16},{24,20},{28,24},{1,29},{... | collective-permute-start | bytes 6920 | tf_op jit(solution)/shard_map/ppermute | solution.py:137
  14.1 7.4 %collective-permute-start = (bf16[9,128]{1,0:T(8,128)(2,1)S(1)}, bf16[9,128]{1,0:T(8,128)(2,1)S(1)}, u32[]{:S(2)}, u32[]{:S(2)}) collective-permute-start(bf16[9,128]{1,0:T(8,128)(2,1)S(1)} %pad_maximum_fusion.9), channel_id=1, source_target_pairs={{0,4},{4,8},{8,12},{12,16},{16,20},{20,24},{24,28},{28,0},{1,5},{5... | collective-permute-start | bytes 6920 | tf_op jit(solution)/shard_map/ppermute | solution.py:135
  14.8 36.2 %collective-permute-start.9 = (bf16[32,3072]{1,0:T(8,128)(2,1)}, bf16[32,3072]{1,0:T(8,128)(2,1)S(1)}, u32[]{:S(2)}, u32[]{:S(2)}) collective-permute-start(bf16[32,3072]{1,0:T(8,128)(2,1)} %fusion.119), channel_id=1, source_target_pairs={{0,24},{1,25},{2,26},{3,27},{4,28},{5,29},{6,30},{7,31},{8,16},{9,... | collective-permute-start | bytes 589832 | tf_op jit(solution)/shard_map/ppermute | solution.py:47
  15.9 35.2 %collective-permute-start.8 = (bf16[32,3072]{1,0:T(8,128)(2,1)}, bf16[32,3072]{1,0:T(8,128)(2,1)}, u32[]{:S(2)}, u32[]{:S(2)}) collective-permute-start(bf16[32,3072]{1,0:T(8,128)(2,1)} %fusion.119), channel_id=1, source_target_pairs={{0,16},{1,17},{2,18},{3,19},{4,20},{5,21},{6,22},{7,23},{8,24},{9,... | collective-permute-start | bytes 589832 | tf_op jit(solution)/shard_map/ppermute | solution.py:47
  15.9 35.2 %collective-permute-start.7 = (bf16[32,3072]{1,0:T(8,128)(2,1)}, bf16[32,3072]{1,0:T(8,128)(2,1)}, u32[]{:S(2)}, u32[]{:S(2)}) collective-permute-start(bf16[32,3072]{1,0:T(8,128)(2,1)} %fusion.119), channel_id=1, source_target_pairs={{0,8},{1,9},{2,10},{3,11},{4,12},{5,13},{6,14},{7,15},{8,0},{9,1},... | collective-permute-start | bytes 589832 | tf_op jit(solution)/shard_map/ppermute | solution.py:47
  21.5 11.3 %collective-permute-start.1 = (bf16[9,128]{1,0:T(8,128)(2,1)S(1)}, bf16[9,128]{1,0:T(8,128)(2,1)S(1)}, u32[]{:S(2)}, u32[]{:S(2)}) collective-permute-start(bf16[9,128]{1,0:T(8,128)(2,1)S(1)} %collective-permute-done), channel_id=1, source_target_pairs={{0,4},{4,8},{8,12},{12,16},{16,20},{20,24},{24,28},{28,0},{1,5},{5... | collective-permute-start | bytes 6920 | tf_op jit(solution)/shard_map/ppermute | solution.py:135
  32.8 6.3 collective-permute-start.2
  32.8 7.4 %collective-permute-start.5 = (bf16[9,128]{1,0:T(8,128)(2,1)S(1)}, bf16[9,128]{1,0:T(8,128)(2,1)S(1)}, u32[]{:S(2)}, u32[]{:S(2)}) collective-permute-start(bf16[9,128]{1,0:T(8,128)(2,1)S(1)} %collective-permute-done.4), channel_id=1, source_target_pairs={{0,28},{4,0},{8,4},{12,8},{16,12},{20,16},{24,20},{28,24},{1,29},{... | collective-permute-start | bytes 6920 | tf_op jit(solution)/shard_map/ppermute | solution.py:137
  39.1 6.3 collective-permute-start.3
  40.3 18.4 %collective-permute-start.19 = (bf16[32,3072]{1,0:T(8,128)(2,1)}, bf16[32,3072]{1,0:T(8,128)(2,1)S(1)}, u32[]{:S(2)}, u32[]{:S(2)}) collective-permute-start(bf16[32,3072]{1,0:T(8,128)(2,1)} %fusion.120), channel_id=1, source_target_pairs={{0,24},{1,25},{2,26},{3,27},{4,28},{5,29},{6,30},{7,31},{8,16},{9,... | collective-permute-start | bytes 589832 | tf_op jit(solution)/shard_map/ppermute | solution.py:47
  45.4 3.6 collective-permute-start.6
  49.0 9.8 %collective-permute-start.18 = (bf16[32,3072]{1,0:T(8,128)(2,1)}, bf16[32,3072]{1,0:T(8,128)(2,1)S(1)}, u32[]{:S(2)}, u32[]{:S(2)}) collective-permute-start(bf16[32,3072]{1,0:T(8,128)(2,1)} %fusion.120), channel_id=1, source_target_pairs={{0,16},{1,17},{2,18},{3,19},{4,20},{5,21},{6,22},{7,23},{8,24},{9,... | collective-permute-start | bytes 589832 | tf_op jit(solution)/shard_map/ppermute | solution.py:47
  51.0 193.5 %copy-start.37 = (f32[1,1024]{1,0:T(1,128)}, f32[1,1024]{1,0:T(1,128)S(1)}, u32[]{:S(2)}) copy-start(f32[1,1024]{1,0:T(1,128)S(1)} %get-tuple-element.56) | copy-start | bytes 12292
  51.0 7.9 %collective-permute-start.17 = (bf16[32,3072]{1,0:T(8,128)(2,1)}, bf16[32,3072]{1,0:T(8,128)(2,1)S(1)}, u32[]{:S(2)}, u32[]{:S(2)}) collective-permute-start(bf16[32,3072]{1,0:T(8,128)(2,1)} %fusion.120), channel_id=1, source_target_pairs={{0,8},{1,9},{2,10},{3,11},{4,12},{5,13},{6,14},{7,15},{8,0},{9,1},... | collective-permute-start | bytes 589832 | tf_op jit(solution)/shard_map/ppermute | solution.py:47
  52.3 20.5 %collective-permute-start.11 = (bf16[4,32,3072]{2,1,0:T(8,128)(2,1)S(1)}, bf16[4,32,3072]{2,1,0:T(8,128)(2,1)S(1)}, u32[]{:S(2)}, u32[]{:S(2)}) collective-permute-start(bf16[4,32,3072]{2,1,0:T(8,128)(2,1)S(1)} %get-tuple-element.53), channel_id=1, source_target_pairs={{0,2},{1,5},{2,0},{3,7},{4,6},{5,1},{6,4},{7,3},{8,10},{9,13},{10,... | collective-permute-start | bytes 2359304 | tf_op jit(solution)/shard_map/ppermute | solution.py:47
  53.9 21.0 %collective-permute-start.10 = (bf16[4,32,3072]{2,1,0:T(8,128)(2,1)S(1)}, bf16[4,32,3072]{2,1,0:T(8,128)(2,1)S(1)}, u32[]{:S(2)}, u32[]{:S(2)}) collective-permute-start(bf16[4,32,3072]{2,1,0:T(8,128)(2,1)S(1)} %get-tuple-element.53), channel_id=1, source_target_pairs={{0,4},{1,3},{2,6},{3,1},{4,0},{5,7},{6,2},{7,5},{8,12},{9,11},{10,... | collective-permute-start | bytes 2359304 | tf_op jit(solution)/shard_map/ppermute | solution.py:47
  58.7 50.0 %collective-permute-start.13 = (bf16[4,32,3072]{2,1,0:T(8,128)(2,1)S(1)}, bf16[4,32,3072]{2,1,0:T(8,128)(2,1)S(1)}, u32[]{:S(2)}, u32[]{:S(2)}) collective-permute-start(bf16[4,32,3072]{2,1,0:T(8,128)(2,1)S(1)} %get-tuple-element.53), channel_id=1, source_target_pairs={{0,1},{1,0},{2,3},{3,2},{4,5},{5,4},{6,7},{7,6},{8,9},{9,8},{10,11... | collective-permute-start | bytes 2359304 | tf_op jit(solution)/shard_map/ppermute | solution.py:47
  59.1 30.6 %collective-permute-start.21 = (bf16[4,32,3072]{2,1,0:T(8,128)(2,1)S(1)}, bf16[4,32,3072]{2,1,0:T(8,128)(2,1)S(1)}, u32[]{:S(2)}, u32[]{:S(2)}) collective-permute-start(bf16[4,32,3072]{2,1,0:T(8,128)(2,1)S(1)} %get-tuple-element.55), channel_id=1, source_target_pairs={{0,2},{1,5},{2,0},{3,7},{4,6},{5,1},{6,4},{7,3},{8,10},{9,13},{10,... | collective-permute-start | bytes 2359304 | tf_op jit(solution)/shard_map/ppermute | solution.py:47
  60.7 29.0 %collective-permute-start.20 = (bf16[4,32,3072]{2,1,0:T(8,128)(2,1)S(1)}, bf16[4,32,3072]{2,1,0:T(8,128)(2,1)S(1)}, u32[]{:S(2)}, u32[]{:S(2)}) collective-permute-start(bf16[4,32,3072]{2,1,0:T(8,128)(2,1)S(1)} %get-tuple-element.55), channel_id=1, source_target_pairs={{0,4},{1,3},{2,6},{3,1},{4,0},{5,7},{6,2},{7,5},{8,12},{9,11},{10,... | collective-permute-start | bytes 2359304 | tf_op jit(solution)/shard_map/ppermute | solution.py:47
  72.8 20.0 %collective-permute-start.12 = (bf16[4,32,3072]{2,1,0:T(8,128)(2,1)S(1)}, bf16[4,32,3072]{2,1,0:T(8,128)(2,1)S(1)}, u32[]{:S(2)}, u32[]{:S(2)}) collective-permute-start(bf16[4,32,3072]{2,1,0:T(8,128)(2,1)S(1)} %collective-permute-done.11), channel_id=1, source_target_pairs={{0,4},{1,3},{2,6},{3,1},{4,0},{5,7},{6,2},{7,5},{8,12},{9,11},{10,... | collective-permute-start | bytes 2359304 | tf_op jit(solution)/shard_map/ppermute | solution.py:47
  74.9 29.1 %collective-permute-start.15 = (bf16[4,32,3072]{2,1,0:T(8,128)(2,1)S(1)}, bf16[4,32,3072]{2,1,0:T(8,128)(2,1)S(1)}, u32[]{:S(2)}, u32[]{:S(2)}) collective-permute-start(bf16[4,32,3072]{2,1,0:T(8,128)(2,1)S(1)} %collective-permute-done.11), channel_id=1, source_target_pairs={{0,1},{1,0},{2,3},{3,2},{4,5},{5,4},{6,7},{7,6},{8,9},{9,8},{10,11... | collective-permute-start | bytes 2359304 | tf_op jit(solution)/shard_map/ppermute | solution.py:47
  89.7 14.4 %collective-permute-start.14 = (bf16[4,32,3072]{2,1,0:T(8,128)(2,1)S(1)}, bf16[4,32,3072]{2,1,0:T(8,128)(2,1)S(1)}, u32[]{:S(2)}, u32[]{:S(2)}) collective-permute-start(bf16[4,32,3072]{2,1,0:T(8,128)(2,1)S(1)} %collective-permute-done.10), channel_id=1, source_target_pairs={{0,1},{1,0},{2,3},{3,2},{4,5},{5,4},{6,7},{7,6},{8,9},{9,8},{10,11... | collective-permute-start | bytes 2359304 | tf_op jit(solution)/shard_map/ppermute | solution.py:47
  89.7 12.1 %collective-permute-start.22 = (bf16[4,32,3072]{2,1,0:T(8,128)(2,1)S(1)}, bf16[4,32,3072]{2,1,0:T(8,128)(2,1)}, u32[]{:S(2)}, u32[]{:S(2)}) collective-permute-start(bf16[4,32,3072]{2,1,0:T(8,128)(2,1)S(1)} %collective-permute-done.21), channel_id=1, source_target_pairs={{0,4},{1,3},{2,6},{3,1},{4,0},{5,7},{6,2},{7,5},{8,12},{9,11},{10,... | collective-permute-start | bytes 2359304 | tf_op jit(solution)/shard_map/ppermute | solution.py:47
  92.8 11.8 %collective-permute-start.25 = (bf16[4,32,3072]{2,1,0:T(8,128)(2,1)S(1)}, bf16[4,32,3072]{2,1,0:T(8,128)(2,1)S(1)}, u32[]{:S(2)}, u32[]{:S(2)}) collective-permute-start(bf16[4,32,3072]{2,1,0:T(8,128)(2,1)S(1)} %collective-permute-done.21), channel_id=1, source_target_pairs={{0,1},{1,0},{2,3},{3,2},{4,5},{5,4},{6,7},{7,6},{8,9},{9,8},{10,11... | collective-permute-start | bytes 2359304 | tf_op jit(solution)/shard_map/ppermute | solution.py:47
  101.8 3.0 collective-permute-start.24
  104.0 2.4 collective-permute-start.23
  104.0 4.5 collective-permute-start.16
  104.7 6.8 %collective-permute-start.26 = (bf16[4,32,3072]{2,1,0:T(8,128)(2,1)}, bf16[4,32,3072]{2,1,0:T(8,128)(2,1)}, u32[]{:S(2)}, u32[]{:S(2)}) collective-permute-start(bf16[4,32,3072]{2,1,0:T(8,128)(2,1)} %collective-permute-done.22), channel_id=1, source_target_pairs={{0,1},{1,0},{2,3},{3,2},{4,5},{5,4},{6,7},{7,6},{8,9},{9,8},{10,11... | collective-permute-start | bytes 2359304 | tf_op jit(solution)/shard_map/ppermute | solution.py:47
  355.2 94.1 %collective-permute-start.36 = (bf16[2,2,4,128,768]{4,3,2,0,1:T(8,128)(2,1)}, bf16[2,2,4,128,768]{4,3,2,0,1:T(8,128)(2,1)}, u32[]{:S(2)}, u32[]{:S(2)}) collective-permute-start(bf16[2,2,4,128,768]{4,3,2,0,1:T(8,128)(2,1)} %bitcast.348), channel_id=1, source_target_pairs={{0,1},{1,0},{2,3},{3,2},{4,5},{5,4},{6,7},{7,6},{8,9},{9,8},{10,11... | collective-permute-start | bytes 9437192 | tf_op jit(solution)/shard_map/ppermute | solution.py:47
  427.4 28.4 %collective-permute-start.27 = (bf16[2,2,4,128,768]{4,3,1,0,2:T(8,128)(2,1)}, bf16[2,2,4,128,768]{4,3,1,0,2:T(8,128)(2,1)}, u32[]{:S(2)}, u32[]{:S(2)}) collective-permute-start(bf16[2,2,4,128,768]{4,3,1,0,2:T(8,128)(2,1)} %fusion.36), channel_id=1, source_target_pairs={{0,1},{1,0},{2,3},{3,2},{4,5},{5,4},{6,7},{7,6},{8,9},{9,8},{10,11... | collective-permute-start | bytes 9437192 | tf_op jit(solution)/shard_map/ppermute | solution.py:47
  454.5 20.7 %collective-permute-start.37 = (bf16[2,4,128,768]{3,2,1,0:T(8,128)(2,1)S(1)}, bf16[2,4,128,768]{3,2,1,0:T(8,128)(2,1)S(1)}, u32[]{:S(2)}, u32[]{:S(2)}) collective-permute-start(bf16[2,4,128,768]{3,2,1,0:T(8,128)(2,1)S(1)} %fusion.68), channel_id=1, source_target_pairs={{0,4},{1,3},{2,6},{3,1},{4,0},{5,7},{6,2},{7,5},{8,12},{9,11},{10,... | collective-permute-start | bytes 4718600 | tf_op jit(solution)/shard_map/ppermute | solution.py:47
  466.0 34.6 %collective-permute-start.28 = (bf16[2,4,128,768]{3,2,0,1:T(8,128)(2,1)S(1)}, bf16[2,4,128,768]{3,2,0,1:T(8,128)(2,1)S(1)}, u32[]{:S(2)}, u32[]{:S(2)}) collective-permute-start(bf16[2,4,128,768]{3,2,0,1:T(8,128)(2,1)S(1)} %fusion.67), channel_id=1, source_target_pairs={{0,4},{1,3},{2,6},{3,1},{4,0},{5,7},{6,2},{7,5},{8,12},{9,11},{10,... | collective-permute-start | bytes 4718600 | tf_op jit(solution)/shard_map/ppermute | solution.py:47
  476.5 94.4 %collective-permute-start.38 = (bf16[4,128,768]{2,1,0:T(8,128)(2,1)}, bf16[4,128,768]{2,1,0:T(8,128)(2,1)}, u32[]{:S(2)}, u32[]{:S(2)}) collective-permute-start(bf16[4,128,768]{2,1,0:T(8,128)(2,1)} %fusion.70), channel_id=1, source_target_pairs={{0,2},{1,5},{2,0},{3,7},{4,6},{5,1},{6,4},{7,3},{8,10},{9,13},{10,... | collective-permute-start | bytes 2359304 | tf_op jit(solution)/shard_map/ppermute | solution.py:47
  502.7 74.8 %collective-permute-start.29 = (bf16[4,128,768]{2,1,0:T(8,128)(2,1)S(1)}, bf16[4,128,768]{2,1,0:T(8,128)(2,1)}, u32[]{:S(2)}, u32[]{:S(2)}) collective-permute-start(bf16[4,128,768]{2,1,0:T(8,128)(2,1)S(1)} %fusion.69), channel_id=1, source_target_pairs={{0,2},{1,5},{2,0},{3,7},{4,6},{5,1},{6,4},{7,3},{8,10},{9,13},{10,... | collective-permute-start | bytes 2359304 | tf_op jit(solution)/shard_map/ppermute | solution.py:47
  572.8 10.5 %collective-permute-start.39 = (bf16[128,768]{1,0:T(8,128)(2,1)S(1)}, bf16[128,768]{1,0:T(8,128)(2,1)S(1)}, u32[]{:S(2)}, u32[]{:S(2)}) collective-permute-start(bf16[128,768]{1,0:T(8,128)(2,1)S(1)} %get-tuple-element.38), channel_id=1, source_target_pairs={{0,8},{1,9},{2,10},{3,11},{4,12},{5,13},{6,14},{7,15},{8,0},{9,1},... | collective-permute-start | bytes 589832 | tf_op jit(solution)/shard_map/ppermute | solution.py:47
  575.7 11.9 %collective-permute-start.41 = (bf16[128,768]{1,0:T(8,128)(2,1)S(1)}, bf16[128,768]{1,0:T(8,128)(2,1)S(1)}, u32[]{:S(2)}, u32[]{:S(2)}) collective-permute-start(bf16[128,768]{1,0:T(8,128)(2,1)S(1)} %get-tuple-element.39), channel_id=1, source_target_pairs={{0,24},{1,25},{2,26},{3,27},{4,28},{5,29},{6,30},{7,31},{8,16},{9,... | collective-permute-start | bytes 589832 | tf_op jit(solution)/shard_map/ppermute | solution.py:47
  577.4 26.5 %collective-permute-start.40 = (bf16[128,768]{1,0:T(8,128)(2,1)S(1)}, bf16[128,768]{1,0:T(8,128)(2,1)S(1)}, u32[]{:S(2)}, u32[]{:S(2)}) collective-permute-start(bf16[128,768]{1,0:T(8,128)(2,1)S(1)} %get-tuple-element.40), channel_id=1, source_target_pairs={{0,16},{1,17},{2,18},{3,19},{4,20},{5,21},{6,22},{7,23},{8,24},{9,... | collective-permute-start | bytes 589832 | tf_op jit(solution)/shard_map/ppermute | solution.py:47
  578.9 26.8 %collective-permute-start.30 = (bf16[128,768]{1,0:T(8,128)(2,1)S(1)}, bf16[128,768]{1,0:T(8,128)(2,1)S(1)}, u32[]{:S(2)}, u32[]{:S(2)}) collective-permute-start(bf16[128,768]{1,0:T(8,128)(2,1)S(1)} %get-tuple-element.41), channel_id=1, source_target_pairs={{0,8},{1,9},{2,10},{3,11},{4,12},{5,13},{6,14},{7,15},{8,0},{9,1},... | collective-permute-start | bytes 589832 | tf_op jit(solution)/shard_map/ppermute | solution.py:47
  581.5 24.7 %collective-permute-start.32 = (bf16[128,768]{1,0:T(8,128)(2,1)S(1)}, bf16[128,768]{1,0:T(8,128)(2,1)S(1)}, u32[]{:S(2)}, u32[]{:S(2)}) collective-permute-start(bf16[128,768]{1,0:T(8,128)(2,1)S(1)} %get-tuple-element.42), channel_id=1, source_target_pairs={{0,24},{1,25},{2,26},{3,27},{4,28},{5,29},{6,30},{7,31},{8,16},{9,... | collective-permute-start | bytes 589832 | tf_op jit(solution)/shard_map/ppermute | solution.py:47
  583.3 28.7 %collective-permute-start.31 = (bf16[128,768]{1,0:T(8,128)(2,1)S(1)}, bf16[128,768]{1,0:T(8,128)(2,1)S(1)}, u32[]{:S(2)}, u32[]{:S(2)}) collective-permute-start(bf16[128,768]{1,0:T(8,128)(2,1)S(1)} %get-tuple-element.43), channel_id=1, source_target_pairs={{0,16},{1,17},{2,18},{3,19},{4,20},{5,21},{6,22},{7,23},{8,24},{9,... | collective-permute-start | bytes 589832 | tf_op jit(solution)/shard_map/ppermute | solution.py:47
  604.0 9.7 %collective-permute-start.44 = (bf16[128,768]{1,0:T(8,128)(2,1)S(1)}, bf16[128,768]{1,0:T(8,128)(2,1)S(1)}, u32[]{:S(2)}, u32[]{:S(2)}) collective-permute-start(bf16[128,768]{1,0:T(8,128)(2,1)S(1)} %fusion.73), channel_id=1, source_target_pairs={{0,3},{1,2},{2,1},{3,0},{4,7},{5,6},{6,5},{7,4},{8,11},{9,10},{10,... | collective-permute-start | bytes 589832 | tf_op jit(solution)/shard_map/ppermute | solution.py:47
  604.5 9.8 %collective-permute-start.43 = (bf16[128,768]{1,0:T(8,128)(2,1)S(1)}, bf16[128,768]{1,0:T(8,128)(2,1)S(1)}, u32[]{:S(2)}, u32[]{:S(2)}) collective-permute-start(bf16[128,768]{1,0:T(8,128)(2,1)S(1)} %fusion.73), channel_id=1, source_target_pairs={{0,1},{1,0},{2,3},{3,2},{4,5},{5,4},{6,7},{7,6},{8,9},{9,8},{10,11... | collective-permute-start | bytes 589832 | tf_op jit(solution)/shard_map/ppermute | solution.py:47
  605.7 9.8 %collective-permute-start.42 = (bf16[128,768]{1,0:T(8,128)(2,1)S(1)}, bf16[128,768]{1,0:T(8,128)(2,1)S(1)}, u32[]{:S(2)}, u32[]{:S(2)}) collective-permute-start(bf16[128,768]{1,0:T(8,128)(2,1)S(1)} %fusion.73), channel_id=1, source_target_pairs={{0,2},{1,3},{2,0},{3,1},{4,6},{5,7},{6,4},{7,5},{8,10},{9,11},{10,... | collective-permute-start | bytes 589832 | tf_op jit(solution)/shard_map/ppermute | solution.py:47
  612.1 10.0 %collective-permute-start.35 = (bf16[128,768]{1,0:T(8,128)(2,1)S(1)}, bf16[128,768]{1,0:T(8,128)(2,1)}, u32[]{:S(2)}, u32[]{:S(2)}) collective-permute-start(bf16[128,768]{1,0:T(8,128)(2,1)S(1)} %fusion.76), channel_id=1, source_target_pairs={{0,3},{1,2},{2,1},{3,0},{4,7},{5,6},{6,5},{7,4},{8,11},{9,10},{10,... | collective-permute-start | bytes 589832 | tf_op jit(solution)/shard_map/ppermute | solution.py:47
  613.0 9.1 %collective-permute-start.34 = (bf16[128,768]{1,0:T(8,128)(2,1)S(1)}, bf16[128,768]{1,0:T(8,128)(2,1)}, u32[]{:S(2)}, u32[]{:S(2)}) collective-permute-start(bf16[128,768]{1,0:T(8,128)(2,1)S(1)} %fusion.76), channel_id=1, source_target_pairs={{0,1},{1,0},{2,3},{3,2},{4,5},{5,4},{6,7},{7,6},{8,9},{9,8},{10,11... | collective-permute-start | bytes 589832 | tf_op jit(solution)/shard_map/ppermute | solution.py:47
  613.7 10.3 %collective-permute-start.33 = (bf16[128,768]{1,0:T(8,128)(2,1)S(1)}, bf16[128,768]{1,0:T(8,128)(2,1)}, u32[]{:S(2)}, u32[]{:S(2)}) collective-permute-start(bf16[128,768]{1,0:T(8,128)(2,1)S(1)} %fusion.76), channel_id=1, source_target_pairs={{0,2},{1,3},{2,0},{3,1},{4,6},{5,7},{6,4},{7,5},{8,10},{9,11},{10,... | collective-permute-start | bytes 589832 | tf_op jit(solution)/shard_map/ppermute | solution.py:47
  (45 other events, 521.3 us)
Sparse Core Ops, SparseCore 0:
  449.4 117.5 all-reduce.1
